TPU v7x, 32 devices: a whole 2x2x4 slice. The times are simulated.
32 devices in a mesh: fsdp: 4 (over x, core), seq: 8 (over z, y).
Axes of the slice: x: 2, y: 2, z: 4, core: 2. Of those that a mesh axis runs over, the one named last changes fastest.
Arguments:
- tokens: bfloat16 [4, 56, 28, 512], P('fsdp', 'seq'), may hold values from -6 to 6
- cotangent: bfloat16 [4, 56, 28, 512], P('fsdp', 'seq'), may hold values from -6 to 6
- region_ids: int32 [56, 28], replicated, may hold values from 0 to 3
- relative_index: int32 [49, 49], replicated, may hold values from 0 to 168, as said below
- first_gain: bfloat16 [512], P('fsdp'), may hold values from 0.5 to 1.5
- first_offset: bfloat16 [512], P('fsdp'), may hold values from -3 to 3
- qkv_weight: bfloat16 [512, 1536], P('fsdp'), may hold values from -0.25 to 0.25
- proj_weight: bfloat16 [512, 512], P('fsdp'), may hold values from -0.75 to 0.75
- bias_table: bfloat16 [16, 169], P('fsdp'), may hold values from -4 to 4
- second_gain: bfloat16 [512], P('fsdp'), may hold values from 0.5 to 1.5
- second_offset: bfloat16 [512], P('fsdp'), may hold values from -3 to 3
- expand_weight: bfloat16 [512, 2048], P('fsdp'), may hold values from -0.25 to 0.25
- reduce_weight: bfloat16 [2048, 512], P('fsdp'), may hold values from -0.125 to 0.125
Outputs:
- output: bfloat16 [4, 56, 28, 512], P('fsdp', 'seq')
- tokens_grad: float32 [4, 56, 28, 512], P('fsdp', 'seq')
- first_gain_grad: float32 [512], P('fsdp')
- first_offset_grad: float32 [512], P('fsdp')
- qkv_weight_grad: float32 [512, 1536], P('fsdp')
- proj_weight_grad: float32 [512, 512], P('fsdp')
- bias_table_grad: float32 [16, 169], P('fsdp')
- second_gain_grad: float32 [512], P('fsdp')
- second_offset_grad: float32 [512], P('fsdp')
- expand_weight_grad: float32 [512, 2048], P('fsdp')
- reduce_weight_grad: float32 [2048, 512], P('fsdp')
Inputs may be any that keep to these rules, and one draw needn't show every extreme that they name: relative_index[i, j] depends only on the row and column offsets between positions i and j of a 7 x 7 window, and distinct offsets give distinct entries.
All inputs are finite; a program needn't handle non-finite values.
Results may differ from a plain program's by a relative error of at most 0.018.
Values may be sent and summed in bfloat16 or wider, within the bound.
A program may use at most 128 MiB of HBM per device.

v0:
```python
import jax
import jax.numpy as jnp
from jax import lax
from jax.sharding import PartitionSpec as P

WS = 7
SHIFT = 3


EPSILON = 1e-05
MASKED = -100.0
SQRT_HALF = 0.7071067811865476
INV_ROOT_TAU = 0.3989422804014327


def layer_norm(values, norm_gain, norm_offset):
    average = jnp.mean(values, axis=-1, keepdims=True)
    centred = values - average
    variance = jnp.mean(centred * centred, axis=-1, keepdims=True)
    inverse = lax.rsqrt(variance + EPSILON)
    normed = centred * inverse
    return (normed * norm_gain + norm_offset, normed, inverse)


def norm_back(upstream, normed, inverse, norm_gain):
    scaled = upstream * norm_gain
    mean_grad = jnp.mean(scaled, axis=-1, keepdims=True)
    second = jnp.mean(scaled * normed, axis=-1, keepdims=True)
    grad_in = inverse * (scaled - mean_grad - normed * second)
    lead_axes = tuple(range(upstream.ndim - 1))
    return (grad_in, jnp.sum(upstream * normed, axis=lead_axes), jnp.sum(upstream, axis=lead_axes))


def gelu_parts(hidden):
    normal_cdf = 0.5 * (1.0 + jax.scipy.special.erf(hidden * SQRT_HALF))
    density = jnp.exp(-0.5 * hidden * hidden) * INV_ROOT_TAU
    return (hidden * normal_cdf, normal_cdf + hidden * density)


def to_windows(field_in, num_heads):
    lead_dims = field_in.shape[:-3]
    num_rows, num_cols, features = field_in.shape[-3:]
    lead_count = len(lead_dims)
    pieces = field_in.reshape(
        lead_dims + (num_rows // WS, WS, num_cols // WS, WS, num_heads, features // num_heads)
    )
    axis_order = tuple(range(lead_count)) + (
        lead_count,
        lead_count + 2,
        lead_count + 4,
        lead_count + 1,
        lead_count + 3,
        lead_count + 5,
    )
    return pieces.transpose(axis_order).reshape(
        lead_dims + (num_rows // WS, num_cols // WS, num_heads, WS * WS, features // num_heads)
    )


def from_windows(window_tiles):
    lead_dims = window_tiles.shape[:-5]
    win_rows, win_cols, num_heads, positions, head_dim = window_tiles.shape[-5:]
    lead_count = len(lead_dims)
    pieces = window_tiles.reshape(lead_dims + (win_rows, win_cols, num_heads, WS, WS, head_dim))
    axis_order = tuple(range(lead_count)) + (
        lead_count,
        lead_count + 3,
        lead_count + 1,
        lead_count + 4,
        lead_count + 2,
        lead_count + 5,
    )
    return pieces.transpose(axis_order).reshape(
        lead_dims + (win_rows * WS, win_cols * WS, num_heads * head_dim)
    )


def make_mask(regions):
    num_rows, num_cols = regions.shape
    region_tiles = (
        regions.reshape(num_rows // WS, WS, num_cols // WS, WS)
        .transpose(0, 2, 1, 3)
        .reshape(num_rows // WS, num_cols // WS, WS * WS)
    )
    same_region = region_tiles[..., :, None] == region_tiles[..., None, :]
    return jnp.where(same_region, 0.0, MASKED).astype(jnp.float32)


def one_hot_index(relative_index, entries):
    return (relative_index[..., None] == jnp.arange(entries, dtype=jnp.int32)).astype(jnp.float32)


def table_bias(table_rows, relative_index):
    onehot = one_hot_index(relative_index, table_rows.shape[-1])
    return jnp.einsum("ijr,hr->hij", onehot, table_rows, precision=lax.Precision.HIGHEST)


def table_grad(bias_grad, relative_index, entries):
    onehot = one_hot_index(relative_index, entries)
    return jnp.einsum("hij,ijr->hr", bias_grad, onehot, precision=lax.Precision.HIGHEST)


def attend_forward(qkv_field, rel_bias, mask_add, num_heads):
    rolled = jnp.roll(qkv_field, -SHIFT, axis=-2)
    window_tiles = to_windows(rolled, num_heads)
    queries, key_tiles, value_tiles = (window_tiles[:, 0], window_tiles[:, 1], window_tiles[:, 2])
    scores = (
        jnp.einsum("bxyhid,bxyhjd->bxyhij", queries, key_tiles, preferred_element_type=jnp.float32)
        + rel_bias
        + mask_add[:, :, None]
    )
    exp_scores = jnp.exp(scores)
    row_total = jnp.sum(exp_scores, axis=-1, keepdims=True)
    attn_probs = (exp_scores / row_total).astype(jnp.bfloat16)
    attn_tiles = jnp.einsum(
        "bxyhij,bxyhjd->bxyhid", attn_probs, value_tiles, preferred_element_type=jnp.float32
    ).astype(jnp.bfloat16)
    field_out = jnp.roll(from_windows(attn_tiles), SHIFT, axis=-2)
    return (field_out, (queries, key_tiles, value_tiles, jnp.log(row_total)))


def attend_backward(grad_field, kept_state, rel_bias, mask_add, num_heads):
    queries, key_tiles, value_tiles, log_total = kept_state
    grad_tiles = to_windows(jnp.roll(grad_field, -SHIFT, axis=-2), num_heads)
    scores = (
        jnp.einsum("bxyhid,bxyhjd->bxyhij", queries, key_tiles, preferred_element_type=jnp.float32)
        + rel_bias
        + mask_add[:, :, None]
    )
    probs_back = jnp.exp(scores - log_total)
    value_grad = jnp.einsum(
        "bxyhij,bxyhid->bxyhjd",
        probs_back.astype(jnp.bfloat16),
        grad_tiles,
        preferred_element_type=jnp.float32,
    )
    prob_grad = jnp.einsum(
        "bxyhid,bxyhjd->bxyhij", grad_tiles, value_tiles, preferred_element_type=jnp.float32
    )
    score_grad = probs_back * (prob_grad - jnp.sum(probs_back * prob_grad, axis=-1, keepdims=True))
    score_low = score_grad.astype(jnp.bfloat16)
    query_scale = queries.shape[-1] ** (-0.5)
    query_grad = (
        jnp.einsum(
            "bxyhij,bxyhjd->bxyhid", score_low, key_tiles, preferred_element_type=jnp.float32
        )
        * query_scale
    )
    key_grad = jnp.einsum(
        "bxyhij,bxyhid->bxyhjd", score_low, queries, preferred_element_type=jnp.float32
    )
    stacked = jnp.stack([query_grad, key_grad, value_grad], axis=1).astype(jnp.bfloat16)
    field_grad = jnp.roll(from_windows(stacked), SHIFT, axis=-2)
    return (field_grad, jnp.sum(score_grad, axis=(0, 1, 2)))


def shards(
    tokens,
    cotangent,
    region_ids,
    relative_index,
    first_gain,
    first_offset,
    qkv_weight,
    proj_weight,
    bias_table,
    second_gain,
    second_offset,
    expand_weight,
    reduce_weight,
):
    gathered = (
        lax.all_gather(first_gain, "fsdp", axis=0, tiled=True),
        lax.all_gather(first_offset, "fsdp", axis=0, tiled=True),
        lax.all_gather(qkv_weight, "fsdp", axis=0, tiled=True),
        lax.all_gather(proj_weight, "fsdp", axis=0, tiled=True),
        lax.all_gather(bias_table, "fsdp", axis=0, tiled=True),
        lax.all_gather(second_gain, "fsdp", axis=0, tiled=True),
        lax.all_gather(second_offset, "fsdp", axis=0, tiled=True),
        lax.all_gather(expand_weight, "fsdp", axis=0, tiled=True),
        lax.all_gather(reduce_weight, "fsdp", axis=0, tiled=True),
    )
    gain_one = gathered[0].astype(jnp.float32)
    offset_one = gathered[1].astype(jnp.float32)
    qkv_full = gathered[2]
    proj_full = gathered[3]
    table_full = gathered[4].astype(jnp.float32)
    gain_two = gathered[5].astype(jnp.float32)
    offset_two = gathered[6].astype(jnp.float32)
    expand_full = gathered[7]
    reduce_full = gathered[8]
    num_images, num_rows, num_cols, width = tokens.shape
    num_heads, entries = table_full.shape
    query_scale = (width // num_heads) ** (-0.5)
    factors = jnp.array([query_scale, 1.0, 1.0], dtype=jnp.float32).reshape(1, 3, 1, 1, 1)
    qkv_cols = qkv_full.reshape(width, 3, width)
    inputs = tokens.astype(jnp.float32)
    normed_one, hat_one, inv_one = layer_norm(inputs, gain_one, offset_one)
    first_low = normed_one.astype(jnp.bfloat16)
    per_device = num_heads // lax.axis_size("seq")
    head_start = lax.axis_index("seq") * per_device
    qkv_local = (
        jnp.einsum("brwc,ctd->btrwd", first_low, qkv_cols, preferred_element_type=jnp.float32)
        * factors
    ).astype(jnp.bfloat16)
    qkv_heads = lax.all_to_all(qkv_local, "seq", split_axis=4, concat_axis=2, tiled=True)
    qkv_heads = jnp.roll(qkv_heads, -SHIFT, axis=2)
    rel_bias = table_bias(
        lax.dynamic_slice_in_dim(table_full, head_start, per_device, 0), relative_index
    )
    mask_add = make_mask(region_ids)
    attn_heads, kept_state = attend_forward(qkv_heads, rel_bias, mask_add, per_device)
    attn_heads = jnp.roll(attn_heads, SHIFT, axis=1)
    attended = lax.all_to_all(attn_heads, "seq", split_axis=1, concat_axis=3, tiled=True)
    middle = inputs + jnp.einsum(
        "brwc,cd->brwd", attended, proj_full, preferred_element_type=jnp.float32
    )
    normed_two, hat_two, inv_two = layer_norm(middle, gain_two, offset_two)
    second_low = normed_two.astype(jnp.bfloat16)
    hidden = jnp.einsum(
        "brwc,cf->brwf", second_low, expand_full, preferred_element_type=jnp.float32
    )
    activated, slope = gelu_parts(hidden)
    act_low = activated.astype(jnp.bfloat16)
    output = (
        middle
        + jnp.einsum("brwf,fc->brwc", act_low, reduce_full, preferred_element_type=jnp.float32)
    ).astype(jnp.bfloat16)
    reduce_grad = jnp.einsum(
        "brwf,brwc->fc", act_low, cotangent, preferred_element_type=jnp.float32
    )
    hidden_grad = (
        jnp.einsum("brwc,fc->brwf", cotangent, reduce_full, preferred_element_type=jnp.float32)
        * slope
    ).astype(jnp.bfloat16)
    expand_grad = jnp.einsum(
        "brwc,brwf->cf", second_low, hidden_grad, preferred_element_type=jnp.float32
    )
    upstream_two = jnp.einsum(
        "brwf,cf->brwc", hidden_grad, expand_full, preferred_element_type=jnp.float32
    )
    back_two, gain_two_grad, offset_two_grad = norm_back(upstream_two, hat_two, inv_two, gain_two)
    middle_grad = cotangent.astype(jnp.float32) + back_two
    middle_low = middle_grad.astype(jnp.bfloat16)
    proj_grad = jnp.einsum(
        "brwc,brwd->cd", attended, middle_low, preferred_element_type=jnp.float32
    )
    attended_grad = jnp.einsum(
        "brwd,cd->brwc", middle_low, proj_full, preferred_element_type=jnp.float32
    ).astype(jnp.bfloat16)
    grad_heads = lax.all_to_all(attended_grad, "seq", split_axis=3, concat_axis=1, tiled=True)
    grad_heads = jnp.roll(grad_heads, -SHIFT, axis=1)
    qkv_grad_heads, bias_grad = attend_backward(
        grad_heads, kept_state, rel_bias, mask_add, per_device
    )
    qkv_grad_heads = jnp.roll(qkv_grad_heads, SHIFT, axis=2)
    qkv_grad = lax.all_to_all(qkv_grad_heads, "seq", split_axis=2, concat_axis=4, tiled=True)
    table_part = table_grad(bias_grad, relative_index, entries)
    table_grads = lax.dynamic_update_slice(
        jnp.zeros((num_heads, entries), jnp.float32), table_part, (head_start, 0)
    )
    qkv_grad_w = jnp.einsum(
        "brwc,btrwd->ctd", first_low, qkv_grad, preferred_element_type=jnp.float32
    ).reshape(width, 3 * width)
    upstream_one = jnp.einsum(
        "btrwd,ctd->brwc", qkv_grad, qkv_cols, preferred_element_type=jnp.float32
    )
    back_one, gain_one_grad, offset_one_grad = norm_back(upstream_one, hat_one, inv_one, gain_one)
    tokens_grad = middle_grad + back_one
    shares = (
        lax.psum_scatter(
            gain_one_grad.astype(jnp.bfloat16), "fsdp", scatter_dimension=0, tiled=True
        ).astype(jnp.float32),
        lax.psum_scatter(
            offset_one_grad.astype(jnp.bfloat16), "fsdp", scatter_dimension=0, tiled=True
        ).astype(jnp.float32),
        lax.psum_scatter(
            qkv_grad_w.astype(jnp.bfloat16), "fsdp", scatter_dimension=0, tiled=True
        ).astype(jnp.float32),
        lax.psum_scatter(
            proj_grad.astype(jnp.bfloat16), "fsdp", scatter_dimension=0, tiled=True
        ).astype(jnp.float32),
        lax.psum_scatter(
            table_grads.astype(jnp.bfloat16), "fsdp", scatter_dimension=0, tiled=True
        ).astype(jnp.float32),
        lax.psum_scatter(
            gain_two_grad.astype(jnp.bfloat16), "fsdp", scatter_dimension=0, tiled=True
        ).astype(jnp.float32),
        lax.psum_scatter(
            offset_two_grad.astype(jnp.bfloat16), "fsdp", scatter_dimension=0, tiled=True
        ).astype(jnp.float32),
        lax.psum_scatter(
            expand_grad.astype(jnp.bfloat16), "fsdp", scatter_dimension=0, tiled=True
        ).astype(jnp.float32),
        lax.psum_scatter(
            reduce_grad.astype(jnp.bfloat16), "fsdp", scatter_dimension=0, tiled=True
        ).astype(jnp.float32),
    )
    totals = (
        lax.psum(shares[0].astype(jnp.bfloat16), "seq").astype(jnp.float32),
        lax.psum(shares[1].astype(jnp.bfloat16), "seq").astype(jnp.float32),
        lax.psum(shares[2].astype(jnp.bfloat16), "seq").astype(jnp.float32),
        lax.psum(shares[3].astype(jnp.bfloat16), "seq").astype(jnp.float32),
        lax.psum(shares[4].astype(jnp.bfloat16), "seq").astype(jnp.float32),
        lax.psum(shares[5].astype(jnp.bfloat16), "seq").astype(jnp.float32),
        lax.psum(shares[6].astype(jnp.bfloat16), "seq").astype(jnp.float32),
        lax.psum(shares[7].astype(jnp.bfloat16), "seq").astype(jnp.float32),
        lax.psum(shares[8].astype(jnp.bfloat16), "seq").astype(jnp.float32),
    )
    qkv_total = totals[2]
    proj_total = totals[3]
    expand_total = totals[7]
    reduce_total = totals[8]
    return (
        output,
        tokens_grad,
        totals[0],
        totals[1],
        qkv_total,
        proj_total,
        totals[4],
        totals[5],
        totals[6],
        expand_total,
        reduce_total,
    )


def solution(mesh):
    placed = (
        P("fsdp", "seq", None, None),
        P("fsdp", "seq", None, None),
        P(),
        P(),
        P("fsdp"),
        P("fsdp"),
        P("fsdp", None),
        P("fsdp", None),
        P("fsdp", None),
        P("fsdp"),
        P("fsdp"),
        P("fsdp", None),
        P("fsdp", None),
    )
    return jax.shard_map(
        shards,
        mesh=mesh,
        in_specs=placed,
        out_specs=(
            P("fsdp", "seq", None, None),
            P("fsdp", "seq", None, None),
            P("fsdp"),
            P("fsdp"),
            P("fsdp", None),
            P("fsdp", None),
            P("fsdp", None),
            P("fsdp"),
            P("fsdp"),
            P("fsdp", None),
            P("fsdp", None),
        ),
        check_vma=False,
    )
```

profile of v0, /device:TPU:0, one launch (start us, length us, event | category | flops | bytes accessed | tf_op | source)
XLA Modules:
  0.0 358.6 jit_solution(13753991665746310214)
XLA Ops:
  10.0 6.2 %all-gather = bf16[4,1,128]{2,1,0:T(2,128)(2,1)S(1)} all-gather(bf16[1,1,128]{2,1,0:T(2,128)(2,1)} %bitcast.275), channel_id=1, replica_groups=mesh['fsdp'=4,'seq'=8] {'fsdp'}, dimensions={0}, use_global_device_ids=true | all-gather | bytes 1280 | tf_op jit(solution)/shard_map/all_gather | solution.py:173
  16.2 5.4 %all-gather.1 = bf16[4,1,128]{2,1,0:T(2,128)(2,1)S(1)} all-gather(bf16[1,1,128]{2,1,0:T(2,128)(2,1)} %bitcast.276), channel_id=1, replica_groups=mesh['fsdp'=4,'seq'=8] {'fsdp'}, dimensions={0}, use_global_device_ids=true | all-gather | bytes 1280 | tf_op jit(solution)/shard_map/all_gather | solution.py:174
  22.0 10.7 %all-gather.9.cloned.1.call-done = bf16[512,1536]{0,1:T(8,128)(2,1)} async-done(((bf16[128,1536]{0,1:T(8,128)(2,1)}), bf16[512,1536]{0,1:T(8,128)(2,1)}) %all-gather.9.cloned.1.call-update) | async-done | bytes 1572880 | tf_op jit(solution)/shard_map/all_gather | solution.py:175
  32.7 2.9 fusion.22
  35.6 3.7 %copy.100 = bf16[1,3,7,28,512]{3,2,1,0,4:T(8,128)(2,1)S(1)} copy(bf16[1,3,7,28,512]{4,3,1,2,0:T(8,128)(2,1)} %fusion.22) | data formatting | bytes 1204224 | tf_op jit(solution)/shard_map/convert_element_type | solution.py:205
  39.4 4.6 %reshape.406 = bf16[8,2,18816]{2,1,0:T(2,128)(2,1)} reshape(bf16[512,1,3,7,28]{4,3,2,1,0:T(8,128)(2,1)S(1)} %bitcast.239) | data formatting | bytes 1204224
  44.0 5.6 %all-to-all-start = ((bf16[8,2,18816]{2,1,0:T(2,128)(2,1)}), bf16[8,2,18816]{2,1,0:T(2,128)(2,1)}, u32[]{:S(2)}, u32[]{:S(2)}) async-start(bf16[8,2,18816]{2,1,0:T(2,128)(2,1)} %reshape.406), calls=%async_computation | async-start | bytes 1204224 | tf_op jit(solution)/shard_map/all_to_all | solution.py:206
  50.4 5.4 %all-gather.2 = bf16[4,4,169]{2,1,0:T(4,128)(2,1)S(1)} all-gather(bf16[1,4,169]{2,1,0:T(4,128)(2,1)S(1)} %bitcast.272), channel_id=1, replica_groups=mesh['fsdp'=4,'seq'=8] {'fsdp'}, dimensions={0}, use_global_device_ids=true | all-gather | bytes 6760 | tf_op jit(solution)/shard_map/all_gather | solution.py:177
  58.4 7.9 %all-to-all-done = bf16[8,2,18816]{2,1,0:T(2,128)(2,1)} async-done(((bf16[8,2,18816]{2,1,0:T(2,128)(2,1)}), bf16[8,2,18816]{2,1,0:T(2,128)(2,1)}, u32[]{:S(2)}, u32[]{:S(2)}) %all-to-all-start) | async-done | bytes 602144 | tf_op jit(solution)/shard_map/all_to_all | solution.py:206
  66.3 4.9 %reshape.407 = bf16[512,1,3,7,28]{4,3,2,1,0:T(8,128)(2,1)S(1)} reshape(bf16[8,2,18816]{2,1,0:T(2,128)(2,1)} %all-to-all-done) | data formatting | bytes 1204224
  71.2 4.5 %copy.101 = bf16[1,3,7,28,8,64]{5,2,4,3,1,0:T(8,128)(2,1)} copy(bf16[1,3,7,28,8,64]{3,2,1,5,4,0:T(8,128)(2,1)S(1)} %bitcast.238) | data formatting | bytes 1204224 | tf_op jit(solution)/shard_map/all_to_all | solution.py:206
  75.7 2.4 all_to_all.51
  80.3 4.3 %reshape.357 = bf16[1,3,8,7,4,7,2,32]{7,6,3,2,5,4,1,0:T(2,128)(2,1)S(1)} reshape(bf16[1,3,56,28,64]{4,2,3,1,0:T(8,128)(2,1)} %fusion.27) | data formatting | bytes 1204224 | tf_op jit(solution)/shard_map/reshape | solution.py:44
  98.6 3.6 %all-to-all-start.1 = ((bf16[8,2,6272]{2,1,0:T(2,128)(2,1)}), bf16[8,2,6272]{2,1,0:T(2,128)(2,1)S(1)}, u32[]{:S(2)}, u32[]{:S(2)}) async-start(bf16[8,2,6272]{2,1,0:T(2,128)(2,1)} %reshape.408), calls=%async_computation.1 | async-start | bytes 401408 | tf_op jit(solution)/shard_map/all_to_all | solution.py:214
  102.2 5.1 %all-gather.3 = bf16[4,1,128]{2,1,0:T(2,128)(2,1)S(1)} all-gather(bf16[1,1,128]{2,1,0:T(2,128)(2,1)S(1)} %bitcast.277), channel_id=1, replica_groups=mesh['fsdp'=4,'seq'=8] {'fsdp'}, dimensions={0}, use_global_device_ids=true | all-gather | bytes 1280 | tf_op jit(solution)/shard_map/all_gather | solution.py:178
  107.3 5.0 %all-gather.4 = bf16[4,1,128]{2,1,0:T(2,128)(2,1)S(1)} all-gather(bf16[1,1,128]{2,1,0:T(2,128)(2,1)S(1)} %bitcast.278), channel_id=1, replica_groups=mesh['fsdp'=4,'seq'=8] {'fsdp'}, dimensions={0}, use_global_device_ids=true | all-gather | bytes 1280 | tf_op jit(solution)/shard_map/all_gather | solution.py:179
  112.4 7.6 %all_gather.31 = bf16[512,512]{1,0:T(8,128)(2,1)S(1)} all-gather(bf16[128,512]{1,0:T(8,128)(2,1)S(1)} %copy-done.22), channel_id=1, replica_groups=mesh['fsdp'=4,'seq'=8] {'fsdp'}, dimensions={0}, use_global_device_ids=true | all-gather | bytes 655360 | tf_op jit(solution)/shard_map/all_gather | solution.py:176
  121.5 4.0 %multiply_convert_fusion = (bf16[7,28,2048]{2,1,0:T(8,128)(2,1)}, f32[7,28,2048]{2,1,0:T(8,128)}) fusion(bf16[512,2048]{1,0:T(8,128)(2,1)} %all-gather.11.cloned.1.call-done, f32[1,7,28,512]{3,2,1,0:T(8,128)S(1)} %get-tuple-element.85, f32[512]{0:T(512)S(1)} %bitcast.270, f32[512]{0:T(512)S(1)} %bitcast.260, f32[7,28]{1,0:T(8,128)S(1)} %add_rsqrt_fusion, ...), kind=kOutput, calls=%fused_computation.25 | convolution fusion | flops 413550592 | bytes 4912672 | tf_op jit(solution)/shard_map/brwc,cf->brwf/dot_general | solution.py:220
  125.5 3.3 fusion.3
  132.2 3.4 bitcast_convert_fusion.1
  136.5 3.3 bitcast_convert_fusion
  144.6 6.0 %all-to-all-start.2 = ((bf16[8,2,6272]{2,1,0:T(2,128)(2,1)}), bf16[8,2,6272]{2,1,0:T(2,128)(2,1)S(1)}, u32[]{:S(2)}, u32[]{:S(2)}) async-start(bf16[8,2,6272]{2,1,0:T(2,128)(2,1)} %reshape.410), calls=%async_computation.2 | async-start | bytes 401408 | tf_op jit(solution)/shard_map/all_to_all | solution.py:251
  152.4 6.7 %all-to-all-done.2 = bf16[8,2,6272]{2,1,0:T(2,128)(2,1)S(1)} async-done(((bf16[8,2,6272]{2,1,0:T(2,128)(2,1)}), bf16[8,2,6272]{2,1,0:T(2,128)(2,1)S(1)}, u32[]{:S(2)}, u32[]{:S(2)}) %all-to-all-start.2) | async-done | bytes 200736 | tf_op jit(solution)/shard_map/all_to_all | solution.py:251
  168.2 2.4 copy.126
  179.9 2.3 reshape.371
  185.1 19.7 %all_to_all.66 = bf16[8,2,18816]{2,1,0:T(2,128)(2,1)S(1)} all-to-all(bf16[8,2,18816]{2,1,0:T(2,128)(2,1)S(1)} %reshape.412), channel_id=1, replica_groups=mesh['fsdp'=4,'seq'=8] {'seq'}, dimensions={0} | all-to-all | bytes 1204224 | tf_op jit(solution)/shard_map/all_to_all | solution.py:257
  212.6 9.0 %reduce-scatter.11.cloned.1.call-done = bf16[512,512]{1,0:T(8,128)(2,1)} async-done(((bf16[2048,512]{1,0:T(8,128)(2,1)}), bf16[512,512]{1,0:T(8,128)(2,1)}) %reduce-scatter.11.cloned.1.call-update) | async-done | bytes 524304 | tf_op jit(solution)/shard_map/reduce_scatter | solution.py:295
  221.6 30.6 %reduce-scatter.5.cloned.1.call-done = bf16[128,1536]{1,0:T(8,128)(2,1)} async-done(((bf16[512,1536]{1,0:T(8,128)(2,1)}), bf16[128,1536]{1,0:T(8,128)(2,1)}) %reduce-scatter.5.cloned.1.call-update) | async-done | bytes 393232 | tf_op jit(solution)/shard_map/reduce_scatter | solution.py:277
  252.2 2.9 fusion.32
  258.6 10.5 %all-reduce.7 = (bf16[512]{0:T(512)(128)(2,1)S(1)}, bf16[512]{0:T(512)(128)(2,1)S(1)}, bf16[16,169]{1,0:T(8,128)(2,1)S(1)}, bf16[512]{0:T(512)(128)(2,1)S(1)}, bf16[512]{0:T(512)(128)(2,1)S(1)}) all-reduce(bf16[512]{0:T(512)(128)(2,1)S(1)} %get-tuple-element.57, ...), channel_id=2, replica_groups=mesh['fsdp'=4,'seq'=8] {'fsdp'}, use_global_device_ids=true, to_apply=%region_11.12.clone | all-reduce | flops 4752 | bytes 19008
  269.4 21.9 %all-reduce.5 = (bf16[128]{0:T(256)(128)(2,1)S(1)}, bf16[128]{0:T(256)(128)(2,1)S(1)}, bf16[4,169]{1,0:T(4,128)(2,1)S(1)}, bf16[128]{0:T(256)(128)(2,1)S(1)}, bf16[128]{0:T(256)(128)(2,1)S(1)}) all-reduce(bf16[128]{0:T(256)(128)(2,1)S(1)} %dynamic-slice.1, ...), channel_id=1, replica_groups=mesh['fsdp'=4,'seq'=8] {'seq'}, use_global_device_ids=true, to_apply=%region_12.13 | all-reduce | flops 1188 | bytes 4752 | tf_op jit(solution)/shard_map/psum | solution.py:300
  295.4 50.3 %all-reduce.10.cloned.1.call-done = (bf16[128,1536]{1,0:T(8,128)(2,1)}, bf16[128,512]{1,0:T(8,128)(2,1)}, bf16[128,2048]{1,0:T(8,128)(2,1)}, bf16[512,512]{1,0:T(8,128)(2,1)}) async-done(((bf16[128,1536]{1,0:T(8,128)(2,1)}, bf16[128,512]{1,0:T(8,128)(2,1)}, bf16[128,2048]{1,0:T(8,128)(2,1)}, bf16[512,512]{1,0:T(8,128)(2,1)}), (bf16[128,1536]{1,0:T(8,128)(2,1)}, bf16[128,512]{1,0:T(8,128)(2,1)}, ...) | async-done | bytes 1572880 | tf_op jit(solution)/shard_map/psum | solution.py:302
  (202 shorter events, 76.0 us)
Async XLA Ops:
  7.2 25.5 %copy-start.34 = (f32[3]{0:T(128)S(1)}, f32[3]{0:T(128)}, u32[]{:S(2)}) copy-start(f32[3]{0:T(128)} %constant.41.clone) | copy-start | bytes 40
  7.2 14.5 %copy-start.7 = (bf16[1,7,28,512]{3,2,1,0:T(8,128)(2,1)S(1)}, bf16[1,7,28,512]{3,2,1,0:T(8,128)(2,1)}, u32[]{:S(2)}) copy-start(bf16[1,7,28,512]{3,2,1,0:T(8,128)(2,1)} %param.14) | copy-start | bytes 602116
  7.2 25.5 %all-gather.9.cloned.1.call-start = ((), (), s32[]{:S(2)}) async-start(), calls=%async_computation.8 | async-start | bytes 1966080 | tf_op jit(solution)/shard_map/all_gather | solution.py:175
  9.2 112.2 %all-gather.11.cloned.1.call-start = ((), (), s32[]{:S(2)}) async-start(), calls=%async_computation.9 | async-start | bytes 2621440 | tf_op jit(solution)/shard_map/all_gather | solution.py:180
  21.6 11.1 %copy-start.26 = (f32[4,1,128]{2,1,0:T(1,128)}, f32[4,1,128]{2,1,0:T(1,128)S(1)}, u32[]{:S(2)}) copy-start(f32[4,1,128]{2,1,0:T(1,128)S(1)} %convert_element_type.190) | copy-start | bytes 6148
  39.4 11.0 %copy-start.25 = (bf16[4,169]{1,0:T(4,128)(2,1)S(1)}, bf16[4,169]{1,0:T(4,128)(2,1)}, u32[]{:S(2)}) copy-start(bf16[4,169]{1,0:T(4,128)(2,1)} %param.22) | copy-start | bytes 4060
  39.4 16.4 %copy-start.31 = (s32[49,49]{1,0:T(8,128)S(1)}, s32[49,49]{1,0:T(8,128)}, u32[]{:S(2)}) copy-start(s32[49,49]{1,0:T(8,128)} %param.17) | copy-start | bytes 28816
  44.0 12.7 %copy-start.23 = (s32[56,28]{0,1:T(8,128)S(1)}, s32[56,28]{0,1:T(8,128)}, u32[]{:S(2)}) copy-start(s32[56,28]{0,1:T(8,128)} %param.16) | copy-start | bytes 18820
  44.0 22.3 %all-to-all-start = ((bf16[8,2,18816]{2,1,0:T(2,128)(2,1)}), bf16[8,2,18816]{2,1,0:T(2,128)(2,1)}, u32[]{:S(2)}, u32[]{:S(2)}) async-start(bf16[8,2,18816]{2,1,0:T(2,128)(2,1)} %reshape.406), calls=%async_computation | async-start | bytes 1204224 | tf_op jit(solution)/shard_map/all_to_all | solution.py:206
  49.6 75.8 %all-gather.13.cloned.1.call-start = ((), (), s32[]{:S(2)}) async-start(), calls=%async_computation.10 | async-start | bytes 2621440 | tf_op jit(solution)/shard_map/all_gather | solution.py:181
  97.3 5.0 %copy-start.29 = (bf16[128]{0:T(256)(128)(2,1)S(1)}, bf16[128]{0:T(256)(128)(2,1)}, u32[]{:S(2)}) copy-start(bf16[128]{0:T(256)(128)(2,1)} %param.23) | copy-start | bytes 772
  97.3 10.0 %copy-start.30 = (bf16[128]{0:T(256)(128)(2,1)S(1)}, bf16[128]{0:T(256)(128)(2,1)}, u32[]{:S(2)}) copy-start(bf16[128]{0:T(256)(128)(2,1)} %param.24) | copy-start | bytes 772
  97.3 15.1 %copy-start.22 = (bf16[128,512]{1,0:T(8,128)(2,1)S(1)}, bf16[128,512]{1,0:T(8,128)(2,1)}, u32[]{:S(2)}) copy-start(bf16[128,512]{1,0:T(8,128)(2,1)} %param.21) | copy-start | bytes 393220
  98.6 21.4 %all-to-all-start.1 = ((bf16[8,2,6272]{2,1,0:T(2,128)(2,1)}), bf16[8,2,6272]{2,1,0:T(2,128)(2,1)S(1)}, u32[]{:S(2)}, u32[]{:S(2)}) async-start(bf16[8,2,6272]{2,1,0:T(2,128)(2,1)} %reshape.408), calls=%async_computation.1 | async-start | bytes 401408 | tf_op jit(solution)/shard_map/all_to_all | solution.py:214
  102.2 110.4 %reduce-scatter.7.cloned.1.call-start = ((), (), s32[]{:S(2)}) async-start(), calls=%async_computation.12 | async-start | bytes 655360 | tf_op jit(solution)/shard_map/reduce_scatter | solution.py:280
  112.4 8.5 %copy-start.8 = (bf16[1,7,28,512]{3,2,1,0:T(8,128)(2,1)S(1)}, bf16[1,7,28,512]{3,2,1,0:T(8,128)(2,1)}, u32[]{:S(2)}) copy-start(bf16[1,7,28,512]{3,2,1,0:T(8,128)(2,1)} %param.14) | copy-start | bytes 602116
  121.5 4.0 %copy-start.18 = (bf16[1,7,28,512]{3,2,1,0:T(8,128)(2,1)S(1)}, bf16[1,7,28,512]{3,2,1,0:T(8,128)(2,1)}, u32[]{:S(2)}) copy-start(bf16[1,7,28,512]{3,2,1,0:T(8,128)(2,1)} %param.15) | copy-start | bytes 602116
  125.4 3.3 copy-start.12
  131.0 8.8 %copy-start.4 = (f32[1,7,28,512]{3,2,1,0:T(8,128)}, f32[1,7,28,512]{3,2,1,0:T(8,128)S(1)}, u32[]{:S(2)}) copy-start(f32[1,7,28,512]{3,2,1,0:T(8,128)S(1)} %fusion.67) | copy-start | bytes 1204228
  132.2 80.4 %reduce-scatter.9.cloned.1.call-start = ((), (), s32[]{:S(2)}) async-start(), calls=%async_computation.13 | async-start | bytes 2621440 | tf_op jit(solution)/shard_map/reduce_scatter | solution.py:292
  135.6 86.0 %reduce-scatter.11.cloned.1.call-start = ((), (), s32[]{:S(2)}) async-start(), calls=%async_computation.14 | async-start | bytes 2621440 | tf_op jit(solution)/shard_map/reduce_scatter | solution.py:295
  144.6 14.5 %all-to-all-start.2 = ((bf16[8,2,6272]{2,1,0:T(2,128)(2,1)}), bf16[8,2,6272]{2,1,0:T(2,128)(2,1)S(1)}, u32[]{:S(2)}, u32[]{:S(2)}) async-start(bf16[8,2,6272]{2,1,0:T(2,128)(2,1)} %reshape.410), calls=%async_computation.2 | async-start | bytes 401408 | tf_op jit(solution)/shard_map/all_to_all | solution.py:251
  150.5 101.6 %reduce-scatter.5.cloned.1.call-start = ((), (), s32[]{:S(2)}) async-start(), calls=%async_computation.11 | async-start | bytes 1966080 | tf_op jit(solution)/shard_map/reduce_scatter | solution.py:277
  163.6 3.1 copy-start.15
  166.8 3.8 %copy-start.14 = (bf16[1,1,8,4,2,49,32]{5,6,4,3,2,1,0:T(8,128)(2,1)S(1)}, bf16[1,1,8,4,2,49,32]{5,6,4,3,2,1,0:T(8,128)(2,1)}, u32[]{:S(2)}) copy-start(bf16[1,1,8,4,2,49,32]{5,6,4,3,2,1,0:T(8,128)(2,1)} %copy.151) | copy-start | bytes 602116
  174.4 3.1 copy-start.10
  210.6 41.6 %copy-start.6 = (bf16[7,28,2048]{2,1,0:T(8,128)(2,1)S(1)}, bf16[7,28,2048]{2,1,0:T(8,128)(2,1)}, u32[]{:S(2)}) copy-start(bf16[7,28,2048]{2,1,0:T(8,128)(2,1)} %get-tuple-element.86) | copy-start | bytes 2408452
  210.6 135.1 %all-reduce.10.cloned.1.call-start = ((), (), s32[]{:S(2)}) async-start(), calls=%async_computation.15 | async-start | bytes 3145728 | tf_op jit(solution)/shard_map/psum | solution.py:302
  252.2 3.1 copy-start.32
  256.3 37.7 %copy-start.5 = (f32[1,7,28,512]{3,2,1,0:T(8,128)S(1)}, f32[1,7,28,512]{3,2,1,0:T(8,128)}, u32[]{:S(2)}) copy-start(f32[1,7,28,512]{3,2,1,0:T(8,128)} %copy-done.4) | copy-start | bytes 1204228
  345.7 3.7 %copy-start.17 = (bf16[128,2048]{1,0:T(8,128)(2,1)S(1)}, bf16[128,2048]{1,0:T(8,128)(2,1)}, u32[]{:S(2)}) copy-start(bf16[128,2048]{1,0:T(8,128)(2,1)} %get-tuple-element.70) | copy-start | bytes 1572868
  345.7 4.7 %copy-start.16 = (bf16[512,512]{1,0:T(8,128)(2,1)S(1)}, bf16[512,512]{1,0:T(8,128)(2,1)}, u32[]{:S(2)}) copy-start(bf16[512,512]{1,0:T(8,128)(2,1)} %get-tuple-element.71) | copy-start | bytes 1572868
  (17 other events, 29.5 us)
Sparse Core Ops, SparseCore 0:
  10.1 22.5 all-gather.8
  34.3 22.5 all-gather.10
  58.5 22.5 all-gather.12
  132.3 22.0 reduce-scatter.6
  156.8 31.1 reduce-scatter.8
  190.4 31.1 reduce-scatter.10
  224.1 27.9 reduce-scatter.4
  256.0 89.6 all-reduce.9
where the time goes:
time: 364 us; the launch traced here: 359 us
  waiting for transfers between devices  117 us (32%)
  blocking collectives  86.9 us (24%)
  local copies, waits for them, and re-layouts  70.6 us (19%)
  matrix products  37 us (10%)
  between operations  16.4 us (5%)
  starting transfers between devices  16 us (4%)
  other arithmetic  15.1 us (4%)
    psum x1, waiting for transfers between devices, shards(): lax.psum(shares[2].astype(jnp.bfloat16), 'seq').astype(jnp.float32)  50.3 us
    reduce_scatter x1, waiting for transfers between devices, shards(): lax.psum_scatter(qkv_grad_w.astype(jnp.bfloat16), 'fsdp', scatter_dimensi...  30.6 us
    unnamed x92, local copies, waits for them, and re-layouts  24.4 us
    psum x1, blocking collectives, shards(): lax.psum(shares[0].astype(jnp.bfloat16), 'seq').astype(jnp.float32)  21.9 us
    all_to_all x1, blocking collectives, shards(): lax.all_to_all(qkv_grad_heads, 'seq', split_axis=2, concat_axis=4, tiled=...  19.7 us
    all_gather x1, waiting for transfers between devices, shards(): lax.all_gather(qkv_weight, 'fsdp', axis=0, tiled=True)  10.7 us
    unnamed x1, blocking collectives  10.5 us
    reduce_scatter x1, waiting for transfers between devices, shards(): lax.psum_scatter(reduce_grad.astype(jnp.bfloat16), 'fsdp', scatter_dimens...  8.98 us
  transfers between devices with their start and end apart: 11, of which 6 were waited for; matrix products, arithmetic and copies ran while one was open for 28% of the time, Pallas kernels for 0%

commit v1 on v0

v1 whole, which is shorter than its diff:
```python
import jax
import jax.numpy as jnp
from jax import lax
from jax.sharding import PartitionSpec as P

WS = 7
SHIFT = 3


EPSILON = 1e-05
MASKED = -100.0
SQRT_HALF = 0.7071067811865476
INV_ROOT_TAU = 0.3989422804014327


def layer_norm(values, norm_gain, norm_offset):
    average = jnp.mean(values, axis=-1, keepdims=True)
    centred = values - average
    variance = jnp.mean(centred * centred, axis=-1, keepdims=True)
    inverse = lax.rsqrt(variance + EPSILON)
    normed = centred * inverse
    return (normed * norm_gain + norm_offset, normed, inverse)


def norm_back(upstream, normed, inverse, norm_gain):
    scaled = upstream * norm_gain
    mean_grad = jnp.mean(scaled, axis=-1, keepdims=True)
    second = jnp.mean(scaled * normed, axis=-1, keepdims=True)
    grad_in = inverse * (scaled - mean_grad - normed * second)
    lead_axes = tuple(range(upstream.ndim - 1))
    return (grad_in, jnp.sum(upstream * normed, axis=lead_axes), jnp.sum(upstream, axis=lead_axes))


def gelu_parts(hidden):
    normal_cdf = 0.5 * (1.0 + jax.scipy.special.erf(hidden * SQRT_HALF))
    density = jnp.exp(-0.5 * hidden * hidden) * INV_ROOT_TAU
    return (hidden * normal_cdf, normal_cdf + hidden * density)


def to_windows(field_in):
    num_rows, num_cols, width = field_in.shape
    pieces = field_in.reshape(num_rows // WS, WS, num_cols // WS, WS, width)
    return pieces.transpose(0, 2, 1, 3, 4).reshape(-1, WS * WS, width)


def from_windows(tiles, num_rows, num_cols):
    pieces = tiles.reshape(num_rows // WS, num_cols // WS, WS, WS, tiles.shape[-1])
    return pieces.transpose(0, 2, 1, 3, 4).reshape(num_rows, num_cols, tiles.shape[-1])


def make_mask(regions):
    num_rows, num_cols = regions.shape
    region_tiles = (
        regions.reshape(num_rows // WS, WS, num_cols // WS, WS)
        .transpose(0, 2, 1, 3)
        .reshape(-1, WS * WS)
    )
    same_region = region_tiles[..., :, None] == region_tiles[..., None, :]
    return jnp.where(same_region, 0.0, MASKED).astype(jnp.float32)


def one_hot_index(relative_index, entries):
    return (relative_index[..., None] == jnp.arange(entries, dtype=jnp.int32)).astype(jnp.bfloat16)


def table_bias(table_low, relative_index):
    onehot = one_hot_index(relative_index, table_low.shape[-1])
    return jnp.einsum("ijr,hr->hij", onehot, table_low, preferred_element_type=jnp.float32)


def table_grad(bias_grad, relative_index, entries):
    onehot = one_hot_index(relative_index, entries).astype(jnp.float32)
    return jnp.einsum("hij,ijr->hr", bias_grad, onehot, precision=lax.Precision.HIGHEST)


def split_heads(tiles, num_heads):
    return tiles.reshape(tiles.shape[0], tiles.shape[1], num_heads, -1).transpose(0, 2, 1, 3)


def join_heads(tiles):
    count, num_heads, positions, head_dim = tiles.shape
    return tiles.transpose(0, 2, 1, 3).reshape(count, positions, num_heads * head_dim)


def mm(form, left, right):
    return jnp.einsum(form, left, right, preferred_element_type=jnp.float32)


def shifted_rows(field, size):
    ring = [(at, (at - 1) % size) for at in range(size)]
    later = lax.ppermute(field[:SHIFT], "seq", ring)
    return jnp.roll(jnp.concatenate([field[SHIFT:], later], axis=0), -SHIFT, axis=1)


def unshifted_rows(field, size):
    ring = [(at, (at + 1) % size) for at in range(size)]
    field = jnp.roll(field, SHIFT, axis=1)
    keep = field.shape[0] - SHIFT
    earlier = lax.ppermute(field[keep:], "seq", ring)
    return jnp.concatenate([earlier, field[:keep]], axis=0)


def shards(
    tokens,
    cotangent,
    region_ids,
    relative_index,
    first_gain,
    first_offset,
    qkv_weight,
    proj_weight,
    bias_table,
    second_gain,
    second_offset,
    expand_weight,
    reduce_weight,
):
    owners = lax.axis_size("fsdp")
    size = lax.axis_size("seq")
    part = first_gain.shape[0]
    small = jnp.concatenate(
        [first_gain, first_offset, second_gain, second_offset, bias_table.reshape(-1)]
    )
    small_full = lax.all_gather(small, "fsdp", axis=0, tiled=False)
    vectors = [
        small_full[:, at * part : (at + 1) * part].reshape(-1).astype(jnp.float32)
        for at in range(4)
    ]
    gain_one, offset_one, gain_two, offset_two = vectors
    table_rows, entries = bias_table.shape
    table_full = small_full[:, 4 * part :].reshape(-1, entries)
    qkv_full = lax.all_gather(qkv_weight, "fsdp", axis=0, tiled=True)
    proj_full = lax.all_gather(proj_weight, "fsdp", axis=0, tiled=True)
    expand_full = lax.all_gather(expand_weight, "fsdp", axis=0, tiled=True)
    reduce_full = lax.all_gather(reduce_weight, "fsdp", axis=0, tiled=True)
    _, num_rows, num_cols, width = tokens.shape
    num_heads = table_full.shape[0]
    query_scale = (width // num_heads) ** (-0.5)

    image_low = to_windows(shifted_rows(tokens[0], size))
    cot = to_windows(shifted_rows(cotangent[0], size))
    inputs = image_low.astype(jnp.float32)
    rel_bias = table_bias(table_full, relative_index)
    regions = lax.dynamic_slice_in_dim(
        region_ids, lax.axis_index("seq") * num_rows, num_rows, 0
    )
    mask_add = make_mask(regions)

    normed_one, hat_one, inv_one = layer_norm(inputs, gain_one, offset_one)
    first_low = normed_one.astype(jnp.bfloat16)
    factors = jnp.concatenate(
        [jnp.full((width,), query_scale, jnp.float32), jnp.ones((2 * width,), jnp.float32)]
    )
    qkv = (mm("wic,cd->wid", first_low, qkv_full) * factors).astype(jnp.bfloat16)
    queries = split_heads(qkv[..., :width], num_heads)
    keys = split_heads(qkv[..., width : 2 * width], num_heads)
    values = split_heads(qkv[..., 2 * width :], num_heads)
    scores = mm("whid,whjd->whij", queries, keys) + rel_bias + mask_add[:, None]
    exp_scores = jnp.exp(scores)
    row_total = jnp.sum(exp_scores, axis=-1, keepdims=True)
    probs = exp_scores / row_total
    probs_low = probs.astype(jnp.bfloat16)
    attended = join_heads(mm("whij,whjd->whid", probs_low, values).astype(jnp.bfloat16))

    middle = inputs + mm("wic,cd->wid", attended, proj_full)
    normed_two, hat_two, inv_two = layer_norm(middle, gain_two, offset_two)
    second_low = normed_two.astype(jnp.bfloat16)
    hidden = mm("wic,cf->wif", second_low, expand_full)
    activated, slope = gelu_parts(hidden)
    act_low = activated.astype(jnp.bfloat16)
    out_tiles = (middle + mm("wif,fc->wic", act_low, reduce_full)).astype(jnp.bfloat16)
    output = unshifted_rows(from_windows(out_tiles, num_rows, num_cols), size)[None]

    def to_owner(grad):
        share = lax.psum_scatter(
            grad.astype(jnp.bfloat16), "fsdp", scatter_dimension=0, tiled=True
        )
        return lax.psum(share, "seq")

    reduce_total = to_owner(mm("wif,wic->fc", act_low, cot))
    hidden_grad = (mm("wic,fc->wif", cot, reduce_full) * slope).astype(jnp.bfloat16)
    expand_total = to_owner(mm("wic,wif->cf", second_low, hidden_grad))
    upstream_two = mm("wif,cf->wic", hidden_grad, expand_full)
    back_two, gain_two_grad, offset_two_grad = norm_back(upstream_two, hat_two, inv_two, gain_two)
    middle_grad = cot.astype(jnp.float32) + back_two
    middle_low = middle_grad.astype(jnp.bfloat16)
    proj_grad = mm("wic,wid->cd", attended, middle_low)

    attended_grad = mm("wid,cd->wic", middle_low, proj_full).astype(jnp.bfloat16)
    grad_tiles = split_heads(attended_grad, num_heads)
    value_grad = mm("whij,whid->whjd", probs_low, grad_tiles)
    prob_grad = mm("whid,whjd->whij", grad_tiles, values)
    score_grad = probs * (prob_grad - jnp.sum(probs * prob_grad, axis=-1, keepdims=True))
    score_low = score_grad.astype(jnp.bfloat16)
    query_grad = mm("whij,whjd->whid", score_low, keys) * query_scale
    key_grad = mm("whij,whid->whjd", score_low, queries)
    qkv_grad = jnp.concatenate(
        [join_heads(grad.astype(jnp.bfloat16)) for grad in (query_grad, key_grad, value_grad)],
        axis=-1,
    )
    table_part = table_grad(jnp.sum(score_grad, axis=0), relative_index, entries)
    qkv_grad_w = mm("wic,wid->cd", first_low, qkv_grad)
    upstream_one = mm("wid,cd->wic", qkv_grad, qkv_full)
    back_one, gain_one_grad, offset_one_grad = norm_back(upstream_one, hat_one, inv_one, gain_one)
    grad_in = from_windows(middle_grad + back_one, num_rows, num_cols)
    tokens_grad = unshifted_rows(grad_in, size)[None]

    small_grads = jnp.concatenate(
        [
            grad.reshape(owners, -1)
            for grad in (gain_one_grad, offset_one_grad, gain_two_grad, offset_two_grad, table_part)
        ],
        axis=1,
    )
    qkv_total = to_owner(qkv_grad_w)
    proj_total = to_owner(proj_grad)
    small_total = lax.psum(small_grads, ("fsdp", "seq"))
    small_total = lax.dynamic_slice_in_dim(small_total, lax.axis_index("fsdp"), 1, 0)[0]
    own = [small_total[at * part : (at + 1) * part] for at in range(4)]
    table_total = small_total[4 * part :].reshape(table_rows, entries)
    wide = jnp.float32
    return (
        output,
        tokens_grad,
        own[0],
        own[1],
        qkv_total.astype(wide),
        proj_total.astype(wide),
        table_total,
        own[2],
        own[3],
        expand_total.astype(wide),
        reduce_total.astype(wide),
    )


def solution(mesh):
    placed = (
        P("fsdp", "seq", None, None),
        P("fsdp", "seq", None, None),
        P(),
        P(),
        P("fsdp"),
        P("fsdp"),
        P("fsdp", None),
        P("fsdp", None),
        P("fsdp", None),
        P("fsdp"),
        P("fsdp"),
        P("fsdp", None),
        P("fsdp", None),
    )
    return jax.shard_map(
        shards,
        mesh=mesh,
        in_specs=placed,
        out_specs=(
            P("fsdp", "seq", None, None),
            P("fsdp", "seq", None, None),
            P("fsdp"),
            P("fsdp"),
            P("fsdp", None),
            P("fsdp", None),
            P("fsdp", None),
            P("fsdp"),
            P("fsdp"),
            P("fsdp", None),
            P("fsdp", None),
        ),
        check_vma=False,
    )
```

time: 364 us -> 322 us (0.88); the launches traced: 359 us -> 322 us
  waiting for transfers between devices: 117 us -> 172 us
  local copies, waits for them, and re-layouts: 70.6 us -> 22.1 us
  blocking collectives: 86.9 us -> 59.8 us
  starting transfers between devices: 16 us -> 10.2 us
  matrix products: 37 us -> 32.1 us
  other arithmetic: 15.1 us -> 10.5 us
    reduce_scatter x4, waiting for transfers between devices: 39.6 us -> 99.5 us  [to_owner(): lax.psum_scatter(grad.astype(jnp.bfloat16), 'fsdp', scatter_dimension=0,...]
    all_gather x6 -> x1, blocking collectives: 34.7 us -> 7.07 us  [shards(): proj_full = lax.all_gather(proj_weight, 'fsdp', axis=0, tiled=True)]
    all_to_all x1 -> x0, blocking collectives: 19.7 us -> none  [shards(): lax.all_to_all(qkv_grad_heads, 'seq', split_axis=2, concat_axis=4, tiled=...]
    psum x1, blocking collectives: 21.9 us -> 41 us  [shards(): small_total = lax.psum(small_grads, ('fsdp', 'seq'))]
    unnamed x92 -> x77, local copies, waits for them, and re-layouts: 24.4 us -> 6.01 us
    all_to_all x3 -> x0, starting transfers between devices: 15.2 us -> none  [the longest x1 5.96 us: shards(): lax.all_to_all(attended_grad, 'seq', split_axis=3, concat_axis=1, tiled=T...]
    all_to_all x3 -> x0, waiting for transfers between devices: 14.6 us -> none  [the longest x1 7.89 us: shards(): lax.all_to_all(qkv_local, 'seq', split_axis=4, concat_axis=2, tiled=True)]
    all_gather x3, waiting for transfers between devices: 10.7 us -> 23.8 us  [the longest x1 20.2 us: shards(): reduce_full = lax.all_gather(reduce_weight, 'fsdp', axis=0, tiled=True)]
  transfers between devices with their start and end apart: 11 -> 12, of which waited for: 6 -> 7; matrix products, arithmetic and copies ran while one was open for 28% -> 13% of each run, Pallas kernels for 0% -> 0%
where the time goes in v1:
time: 322 us
  waiting for transfers between devices  172 us (53%)
  blocking collectives  59.8 us (19%)
  matrix products  32.1 us (10%)
  local copies, waits for them, and re-layouts  22.1 us (7%)
  between operations  15.5 us (5%)
  other arithmetic  10.5 us (3%)
  starting transfers between devices  10.2 us (3%)
    reduce_scatter x4, waiting for transfers between devices, to_owner(): lax.psum_scatter(grad.astype(jnp.bfloat16), 'fsdp', scatter_dimension=0,...  99.5 us
    psum x1, waiting for transfers between devices, to_owner(): return lax.psum(share, 'seq')  46.8 us
    psum x1, blocking collectives, shards(): small_total = lax.psum(small_grads, ('fsdp', 'seq'))  41 us
    dot_general x17, matrix products, mm(): return jnp.einsum(form, left, right, preferred_element_type=jnp.float32)  28.2 us
    all_gather x1, waiting for transfers between devices, shards(): reduce_full = lax.all_gather(reduce_weight, 'fsdp', axis=0, tiled=True)  20.2 us
    unnamed x1, blocking collectives  11.7 us
    all_gather x1, blocking collectives, shards(): proj_full = lax.all_gather(proj_weight, 'fsdp', axis=0, tiled=True)  7.07 us
    ppermute x2, starting transfers between devices, shifted_rows(): later = lax.ppermute(field[:SHIFT], 'seq', ring)  6.64 us
  transfers between devices with their start and end apart: 12, of which 7 were waited for; matrix products, arithmetic and copies ran while one was open for 13% of the time, Pallas kernels for 0%

profile of v1, /device:TPU:0, one launch (start us, length us, event | category | flops | bytes accessed | tf_op | source)
XLA Modules:
  0.0 321.8 jit_solution(5915184115103023686)
XLA Ops:
  9.8 6.1 %collective-permute-start.2 = (bf16[3,28,512]{2,0,1:T(4,128)(2,1)S(1)}, bf16[3,28,512]{2,0,1:T(4,128)(2,1)S(1)}, u32[]{:S(2)}, u32[]{:S(2)}) collective-permute-start(bf16[3,28,512]{2,0,1:T(4,128)(2,1)S(1)} %bitcast.198), channel_id=1, source_target_pairs={{0,7},{1,0},{2,1},{3,2},{4,3},{5,4},{6,5},{7,6},{8,15},{9,8},{10,9... | collective-permute-start | bytes 258056 | tf_op jit(solution)/shard_map/ppermute | solution.py:91
  20.3 11.7 %all-reduce = bf16[4752]{0:T(1024)(128)(2,1)S(1)} all-reduce(bf16[4752]{0:T(1024)(128)(2,1)S(1)} %dynamic-update-slice), channel_id=2, replica_groups=mesh['fsdp'=4,'seq'=8] {'fsdp'}, use_global_device_ids=true, to_apply=%add | all-reduce | flops 4752 | bytes 19008
  33.4 7.1 %all_gather.21 = bf16[512,512]{1,0:T(8,128)(2,1)S(1)} all-gather(bf16[128,512]{1,0:T(8,128)(2,1)S(1)} %copy-done.17), channel_id=1, replica_groups=mesh['fsdp'=4,'seq'=8] {'fsdp'}, dimensions={0}, use_global_device_ids=true | all-gather | bytes 655360 | tf_op jit(solution)/shard_map/all_gather | solution.py:133
  44.0 2.2 fusion.3
  48.7 2.0 fusion.31
  50.7 1.5 convolution_convert_fusion.2
  52.9 3.5 %all-gather.7.cloned.1.call-done = bf16[512,2048]{1,0:T(8,128)(2,1)} async-done(((bf16[128,2048]{1,0:T(8,128)(2,1)}), bf16[512,2048]{1,0:T(8,128)(2,1)}) %all-gather.7.cloned.1.call-update) | async-done | bytes 2097168 | tf_op jit(solution)/shard_map/all_gather | solution.py:134
  56.4 3.9 %multiply_convert_fusion = (bf16[4,49,2048]{2,1,0:T(8,128)(2,1)}, f32[4,49,2048]{2,1,0:T(8,128)}) fusion(bf16[512,2048]{1,0:T(8,128)(2,1)} %all-gather.7.cloned.1.call-done, f32[4,49,512]{2,1,0:T(8,128)S(1)} %get-tuple-element.59, f32[512]{0:T(512)S(1)} %get-tuple-element.55, f32[512]{0:T(512)S(1)} %get-tuple-element.54, f32[4,49]{1,0:T(4,128)S(1)} %add_rsqrt_fusion.1, ...), kind=kOutput, calls=%fused_computation.25 | convolution fusion | flops 413550592 | bytes 4912672 | tf_op jit(solution)/shard_map/wic,cf->wif/dot_general | solution.py:86
  60.3 20.2 %all-gather.9.cloned.1.call-done = bf16[2048,512]{1,0:T(8,128)(2,1)} async-done(((bf16[512,512]{1,0:T(8,128)(2,1)}), bf16[2048,512]{1,0:T(8,128)(2,1)}) %all-gather.9.cloned.1.call-update) | async-done | bytes 2097168 | tf_op jit(solution)/shard_map/all_gather | solution.py:135
  80.6 3.4 %fusion.4 = bf16[4,49,2048]{2,1,0:T(8,128)(2,1)S(1)} fusion(bf16[2048,512]{1,0:T(8,128)(2,1)} %all-gather.9.cloned.1.call-done, f32[4,49,2048]{2,1,0:T(8,128)} %get-tuple-element.61, bf16[4,49,512]{2,0,1:T(4,128)(2,1)} %bitcast.193), kind=kOutput, calls=%fused_computation.11 | convolution fusion | flops 415055872 | bytes 4706304 | tf_op jit(solution)/shard_map/wic,fc->wif/dot_general | solution.py:86
  86.4 1.1 fusion.22
  88.6 1.3 reshape.217
  89.8 2.1 copy.107
  91.9 1.4 convolution_convert_fusion
  93.3 1.9 multiply_reduce_fusion
  95.5 1.3 copy.114
  96.8 2.7 fusion.32
  101.5 2.0 fusion
  103.5 2.2 bitcast_convert_fusion.1
  106.9 2.1 bitcast_convert_fusion
  109.1 2.4 fusion.26
  113.6 1.5 collective-permute-start.1
  115.4 1.7 reduce-scatter.7.cloned.1.call-done
  117.1 30.5 %reduce-scatter.5.cloned.1.call-done = bf16[128,1536]{1,0:T(8,128)(2,1)} async-done(((bf16[512,1536]{1,0:T(8,128)(2,1)}), bf16[128,1536]{1,0:T(8,128)(2,1)}) %reduce-scatter.5.cloned.1.call-update) | async-done | bytes 393232 | tf_op jit(solution)/shard_map/reduce_scatter | solution.py:175
  147.5 33.6 %reduce-scatter.9.cloned.1.call-done = bf16[128,2048]{1,0:T(8,128)(2,1)} async-done(((bf16[512,2048]{1,0:T(8,128)(2,1)}), bf16[128,2048]{1,0:T(8,128)(2,1)}) %reduce-scatter.9.cloned.1.call-update) | async-done | bytes 524304 | tf_op jit(solution)/shard_map/reduce_scatter | solution.py:175
  181.1 33.7 %reduce-scatter.11.cloned.1.call-done = bf16[512,512]{1,0:T(8,128)(2,1)} async-done(((bf16[2048,512]{1,0:T(8,128)(2,1)}), bf16[512,512]{1,0:T(8,128)(2,1)}) %reduce-scatter.11.cloned.1.call-update) | async-done | bytes 524304 | tf_op jit(solution)/shard_map/reduce_scatter | solution.py:175
  216.1 1.5 collective-permute-start.3
  217.7 41.0 %psum.35 = f32[4,1188]{1,0:T(4,128)S(1)} all-reduce(f32[4,1188]{1,0:T(4,128)S(1)} %constant_dynamic-update-slice_fusion), channel_id=1, replica_groups=mesh['fsdp'=4,'seq'=8] {'fsdp','seq'}, use_global_device_ids=true, to_apply=%region_15.16 | all-reduce | flops 4752 | bytes 38016 | tf_op jit(solution)/shard_map/psum | solution.py:217
  261.1 1.2 copy.121
  262.2 46.8 %all-reduce.4.cloned.1.call-done = (bf16[128,1536]{1,0:T(8,128)(2,1)}, bf16[128,512]{1,0:T(8,128)(2,1)}, bf16[128,2048]{1,0:T(8,128)(2,1)}, bf16[512,512]{1,0:T(8,128)(2,1)}) async-done(((bf16[128,1536]{1,0:T(8,128)(2,1)}, bf16[128,512]{1,0:T(8,128)(2,1)}, bf16[128,2048]{1,0:T(8,128)(2,1)}, bf16[512,512]{1,0:T(8,128)(2,1)}), (bf16[128,1536]{1,0:T(8,128)(2,1)}, bf16[128,512]{1,0:T(8,128)(2,1)}, ...) | async-done | bytes 1572880 | tf_op jit(solution)/shard_map/psum | solution.py:178
  309.1 1.7 convert_element_type.181
  310.8 2.0 convert_element_type.179
  (176 shorter events, 29.1 us)
Async XLA Ops:
  7.2 25.0 %copy-start = (s32[56,28]{0,1:T(8,128)S(1)}, s32[56,28]{0,1:T(8,128)}, u32[]{:S(2)}) copy-start(s32[56,28]{0,1:T(8,128)} %param.15) | copy-start | bytes 18820
  7.2 10.4 %copy-start.26 = (u32[32]{0:T(128)S(1)}, u32[32]{0:T(128)}, u32[]{:S(2)}) copy-start(u32[32]{0:T(128)} %constant.51) | copy-start | bytes 388
  7.2 10.3 %copy-start.18 = (bf16[4,169]{1,0:T(4,128)(2,1)S(1)}, bf16[4,169]{1,0:T(4,128)(2,1)}, u32[]{:S(2)}) copy-start(bf16[4,169]{1,0:T(4,128)(2,1)} %param.21) | copy-start | bytes 4060
  7.2 11.7 %copy-start.19 = (bf16[128]{0:T(256)(128)(2,1)S(1)}, bf16[128]{0:T(256)(128)(2,1)}, u32[]{:S(2)}) copy-start(bf16[128]{0:T(256)(128)(2,1)} %param.17) | copy-start | bytes 772
  7.2 11.9 %copy-start.20 = (bf16[128]{0:T(256)(128)(2,1)S(1)}, bf16[128]{0:T(256)(128)(2,1)}, u32[]{:S(2)}) copy-start(bf16[128]{0:T(256)(128)(2,1)} %param.18) | copy-start | bytes 772
  7.2 12.1 %copy-start.21 = (bf16[128]{0:T(256)(128)(2,1)S(1)}, bf16[128]{0:T(256)(128)(2,1)}, u32[]{:S(2)}) copy-start(bf16[128]{0:T(256)(128)(2,1)} %param.22) | copy-start | bytes 772
  7.2 12.3 %copy-start.22 = (bf16[128]{0:T(256)(128)(2,1)S(1)}, bf16[128]{0:T(256)(128)(2,1)}, u32[]{:S(2)}) copy-start(bf16[128]{0:T(256)(128)(2,1)} %param.23) | copy-start | bytes 772
  7.3 25.4 %copy-start.24 = (s32[49,49]{1,0:T(8,128)S(1)}, s32[49,49]{1,0:T(8,128)}, u32[]{:S(2)}) copy-start(s32[49,49]{1,0:T(8,128)} %param.16) | copy-start | bytes 28816
  7.3 26.1 %copy-start.17 = (bf16[128,512]{1,0:T(8,128)(2,1)S(1)}, bf16[128,512]{1,0:T(8,128)(2,1)}, u32[]{:S(2)}) copy-start(bf16[128,512]{1,0:T(8,128)(2,1)} %param.20) | copy-start | bytes 393220
  7.3 36.7 %all-gather.5.cloned.1.call-start = ((), (), s32[]{:S(2)}) async-start(), calls=%async_computation.4 | async-start | bytes 1966080 | tf_op jit(solution)/shard_map/all_gather | solution.py:132
  8.0 48.4 %all-gather.7.cloned.1.call-start = ((), (), s32[]{:S(2)}) async-start(), calls=%async_computation.5 | async-start | bytes 2621440 | tf_op jit(solution)/shard_map/all_gather | solution.py:134
  8.8 71.8 %all-gather.9.cloned.1.call-start = ((), (), s32[]{:S(2)}) async-start(), calls=%async_computation.6 | async-start | bytes 2621440 | tf_op jit(solution)/shard_map/all_gather | solution.py:135
  9.7 30.8 %slice-start.1 = ((bf16[1,7,28,512]{3,2,1,0:T(8,128)(2,1)}), bf16[1,4,28,512]{3,2,1,0:T(8,128)(2,1)S(1)}, s32[]{:S(2)}) async-start(bf16[1,7,28,512]{3,2,1,0:T(8,128)(2,1)} %param.13), calls=%async_computation.13 | async-start | bytes 262144 | tf_op jit(solution)/shard_map/slice | solution.py:92
  9.8 30.8 %slice-start = ((bf16[1,7,28,512]{3,2,1,0:T(8,128)(2,1)}), bf16[1,4,28,512]{3,2,1,0:T(8,128)(2,1)S(1)}, s32[]{:S(2)}) async-start(bf16[1,7,28,512]{3,2,1,0:T(8,128)(2,1)} %param.14), calls=%async_computation.12 | async-start | bytes 262144 | tf_op jit(solution)/shard_map/slice | solution.py:92
  9.8 31.9 %collective-permute-start.2 = (bf16[3,28,512]{2,0,1:T(4,128)(2,1)S(1)}, bf16[3,28,512]{2,0,1:T(4,128)(2,1)S(1)}, u32[]{:S(2)}, u32[]{:S(2)}) collective-permute-start(bf16[3,28,512]{2,0,1:T(4,128)(2,1)S(1)} %bitcast.198), channel_id=1, source_target_pairs={{0,7},{1,0},{2,1},{3,2},{4,3},{5,4},{6,5},{7,6},{8,15},{9,8},{10,9... | collective-permute-start | bytes 258056 | tf_op jit(solution)/shard_map/ppermute | solution.py:91
  16.9 25.8 %collective-permute-start = (bf16[3,28,512]{2,0,1:T(4,128)(2,1)S(1)}, bf16[3,28,512]{2,0,1:T(4,128)(2,1)S(1)}, u32[]{:S(2)}, u32[]{:S(2)}) collective-permute-start(bf16[3,28,512]{2,0,1:T(4,128)(2,1)S(1)} %bitcast.197), channel_id=1, source_target_pairs={{0,7},{1,0},{2,1},{3,2},{4,3},{5,4},{6,5},{7,6},{8,15},{9,8},{10,9... | collective-permute-start | bytes 258056 | tf_op jit(solution)/shard_map/ppermute | solution.py:91
  17.5 99.6 %reduce-scatter.7.cloned.1.call-start = ((), (), s32[]{:S(2)}) async-start(), calls=%async_computation.8 | async-start | bytes 655360 | tf_op jit(solution)/shard_map/reduce_scatter | solution.py:175
  43.9 2.3 copy-start.4
  46.6 4.1 %copy-start.9 = (bf16[4,49,512]{1,2,0:T(8,128)(2,1)}, bf16[4,49,512]{1,2,0:T(8,128)(2,1)S(1)}, u32[]{:S(2)}) copy-start(bf16[4,49,512]{1,2,0:T(8,128)(2,1)S(1)} %copy.135) | copy-start | bytes 602116
  80.6 3.4 %copy-start.8 = (bf16[512,2048]{1,0:T(8,128)(2,1)S(1)}, bf16[512,2048]{1,0:T(8,128)(2,1)}, u32[]{:S(2)}) copy-start(bf16[512,2048]{1,0:T(8,128)(2,1)} %all-gather.7.cloned.1.call-done) | copy-start | bytes 6291460
  89.8 3.5 %copy-start.3 = (bf16[4,49,512]{1,2,0:T(8,128)(2,1)S(1)}, bf16[4,49,512]{1,2,0:T(8,128)(2,1)}, u32[]{:S(2)}) copy-start(bf16[4,49,512]{1,2,0:T(8,128)(2,1)} %copy.134) | copy-start | bytes 602116
  95.3 52.2 %reduce-scatter.5.cloned.1.call-start = ((), (), s32[]{:S(2)}) async-start(), calls=%async_computation.7 | async-start | bytes 1966080 | tf_op jit(solution)/shard_map/reduce_scatter | solution.py:175
  96.8 2.7 copy-start.10
  103.5 77.6 %reduce-scatter.9.cloned.1.call-start = ((), (), s32[]{:S(2)}) async-start(), calls=%async_computation.9 | async-start | bytes 2621440 | tf_op jit(solution)/shard_map/reduce_scatter | solution.py:175
  105.7 109.1 %reduce-scatter.11.cloned.1.call-start = ((), (), s32[]{:S(2)}) async-start(), calls=%async_computation.10 | async-start | bytes 2621440 | tf_op jit(solution)/shard_map/reduce_scatter | solution.py:175
  109.0 200.1 %all-reduce.4.cloned.1.call-start = ((), (), s32[]{:S(2)}) async-start(), calls=%async_computation.11 | async-start | bytes 3145728 | tf_op jit(solution)/shard_map/psum | solution.py:178
  109.1 2.6 copy-start.23
  113.4 101.5 %copy-start.25 = (s32[49,49]{1,0:T(8,128)S(1)}, s32[49,49]{1,0:T(8,128)}, u32[]{:S(2)}) copy-start(s32[49,49]{1,0:T(8,128)} %param.16) | copy-start | bytes 28816
  113.6 146.5 %collective-permute-start.1 = (bf16[3,28,512]{2,0,1:T(4,128)(2,1)S(1)}, bf16[3,28,512]{2,0,1:T(4,128)(2,1)S(1)}, u32[]{:S(2)}, u32[]{:S(2)}) collective-permute-start(bf16[3,28,512]{2,0,1:T(4,128)(2,1)S(1)} %fusion.51), channel_id=1, source_target_pairs={{0,1},{1,2},{2,3},{3,4},{4,5},{5,6},{6,7},{7,0},{8,9},{9,10},{10,1... | collective-permute-start | bytes 258056 | tf_op jit(solution)/shard_map/ppermute | solution.py:99
  216.1 44.8 %collective-permute-start.3 = (f32[3,28,512]{2,0,1:T(4,128)S(1)}, f32[3,28,512]{2,0,1:T(4,128)S(1)}, u32[]{:S(2)}, u32[]{:S(2)}) collective-permute-start(f32[3,28,512]{2,0,1:T(4,128)S(1)} %fusion.42), channel_id=1, source_target_pairs={{0,1},{1,2},{2,3},{3,4},{4,5},{5,6},{6,7},{7,0},{8,9},{9,10},{10,1... | collective-permute-start | bytes 516104 | tf_op jit(solution)/shard_map/ppermute | solution.py:99
  309.1 3.7 %copy-start.16 = (bf16[128,2048]{1,0:T(8,128)(2,1)S(1)}, bf16[128,2048]{1,0:T(8,128)(2,1)}, u32[]{:S(2)}) copy-start(bf16[128,2048]{1,0:T(8,128)(2,1)} %get-tuple-element.43) | copy-start | bytes 1572868
  309.1 4.7 %copy-start.15 = (bf16[512,512]{1,0:T(8,128)(2,1)S(1)}, bf16[512,512]{1,0:T(8,128)(2,1)}, u32[]{:S(2)}) copy-start(bf16[512,512]{1,0:T(8,128)(2,1)} %get-tuple-element.44) | copy-start | bytes 1572868
  (12 other events, 17.0 us)
Sparse Core Ops, SparseCore 0:
  9.6 22.5 all-gather.4
  33.8 22.5 all-gather.6
  58.0 22.5 all-gather.8
  95.4 21.6 reduce-scatter.6
  119.4 28.0 reduce-scatter.4
  149.9 31.1 reduce-scatter.8
  183.6 31.1 reduce-scatter.10
  218.7 90.3 all-reduce.3

commit v2 on v1

--- a/solution.py
+++ b/solution.py
@@ -1,6 +1,10 @@
+import functools
+
 import jax
 import jax.numpy as jnp
 from jax import lax
+from jax.experimental import pallas as pl
+from jax.experimental.pallas import tpu as pltpu
 from jax.sharding import PartitionSpec as P
 
 WS = 7
@@ -84,6 +88,160 @@
 
 def mm(form, left, right):
     return jnp.einsum(form, left, right, preferred_element_type=jnp.float32)
+
+
+def reduce_kernel(count, pairs, halves, *refs):
+    grads, outs = refs[:count], refs[count : 2 * count]
+    rest = refs[2 * count :]
+    stages = [rest[at * count : (at + 1) * count] for at in range(7)]
+    first_in, first_sum, second_in, second_sum, third_in, third_sum, fourth_in = stages
+    send_sem, recv_sem = rest[7 * count :]
+    place, line = lax.axis_index("fsdp"), lax.axis_index("seq")
+    pair, core = place // 2, place % 2
+    half, side = line // 2, line % 2
+    mesh_id = pl.DeviceIdType.MESH
+
+    def on_fsdp(pair_at, core_at):
+        return {"fsdp": pair_at * 2 + core_at, "seq": line}
+
+    def on_seq(half_at, side_at):
+        return {"fsdp": place, "seq": half_at * 2 + side_at}
+
+    pair_peers = [(pair + step) % pairs for step in range(1, pairs)]
+    half_peers = [(half + step) % halves for step in range(1, halves)]
+    everyone = [on_fsdp(pair, 1 - core)] + [on_fsdp(peer, core) for peer in pair_peers]
+    everyone += [on_seq(half, 1 - side)] + [on_seq(peer, side) for peer in half_peers]
+    barrier = pltpu.get_barrier_semaphore()
+    for device in everyone:
+        pl.semaphore_signal(barrier, inc=1, device_id=device, device_id_type=mesh_id)
+    pl.semaphore_wait(barrier, len(everyone))
+
+    started = {}
+    used = [0] * count
+
+    def send(stage, at, source, target, device):
+        slot = used[at]
+        used[at] += 1
+        copy = pltpu.make_async_remote_copy(
+            src_ref=source,
+            dst_ref=target,
+            send_sem=send_sem.at[at, slot],
+            recv_sem=recv_sem.at[at, slot],
+            device_id=device,
+            device_id_type=mesh_id,
+        )
+        copy.start()
+        started.setdefault((stage, at), []).append(copy)
+
+    def arrived(stage, at):
+        for copy in started[(stage, at)]:
+            copy.wait_recv()
+
+    def add(target, terms, low):
+        total = terms[0].astype(jnp.float32)
+        for term in terms[1:]:
+            total = total + term.astype(jnp.float32)
+        target[low] = total.astype(target.dtype)
+
+    def sum_pair(at, pair_at):
+        @pl.loop(0, 2 * halves)
+        def _(piece):
+            mine = grads[at][pair_at, core, piece // 2, piece % 2]
+            came = first_in[at][pair_at, piece // 2, piece % 2]
+            add(first_sum[at], [mine, came], (pair_at, piece // 2, piece % 2))
+
+    def sum_side(at, side_at):
+        @pl.loop(0, halves)
+        def _(piece):
+            terms = [first_sum[at][pair, piece, side_at]]
+            terms += [second_in[at][step, piece, side_at] for step in range(pairs - 1)]
+            add(second_sum[at], terms, (piece, side_at))
+
+    def stage_first(at):
+        send(0, at, grads[at].at[:, 1 - core], first_in[at], on_fsdp(pair, 1 - core))
+
+    def stage_second(at):
+        arrived(0, at)
+        for step, peer in enumerate(pair_peers):
+            sum_pair(at, peer)
+            send(1, at, first_sum[at].at[peer], second_in[at].at[step], on_fsdp(peer, core))
+        sum_pair(at, pair)
+
+    def stage_third(at):
+        arrived(1, at)
+        sum_side(at, 1 - side)
+        send(2, at, second_sum[at].at[:, 1 - side], third_in[at], on_seq(half, 1 - side))
+        sum_side(at, side)
+
+    def stage_fourth(at):
+        arrived(2, at)
+
+        @pl.loop(0, halves)
+        def _(piece):
+            add(third_sum[at], [second_sum[at][piece, side], third_in[at][piece]], (piece,))
+
+        for step, peer in enumerate(half_peers):
+            send(3, at, third_sum[at].at[peer], fourth_in[at].at[step], on_seq(peer, side))
+
+    def stage_fifth(at):
+        arrived(3, at)
+        terms = [third_sum[at][half]] + [fourth_in[at][step] for step in range(halves - 1)]
+        add(outs[at], terms, (half, side))
+        own = outs[at].at[half, side]
+        for peer in half_peers:
+            send(4, at, own, own, on_seq(peer, side))
+
+    def stage_sixth(at):
+        arrived(4, at)
+        own = outs[at].at[:, side]
+        send(5, at, own, own, on_seq(half, 1 - side))
+
+    for at in range(count):
+        stage_first(at)
+    later = (stage_second, stage_third, stage_fourth, stage_fifth, stage_sixth)
+    for tick in range(count + len(later) - 1):
+        for lag, stage in enumerate(later):
+            if 0 <= tick - lag < count:
+                stage(tick - lag)
+    for at in range(count):
+        arrived(5, at)
+    for copies in started.values():
+        for copy in copies:
+            copy.wait_send()
+
+
+def reduce_all(grads, owners, size):
+    pairs, halves, count = owners // 2, size // 2, len(grads)
+    blocks, shapes = [], []
+    for grad in grads:
+        rows, columns = grad.shape[0] // (owners * size), grad.shape[1]
+        if rows % 16:
+            rows, columns = rows * columns // 128, 128
+        shapes.append((rows, columns))
+        blocks.append(grad.reshape(pairs, 2, halves, 2, rows, columns))
+    leads = [
+        (pairs, halves, 2),
+        (pairs, halves, 2),
+        (max(pairs - 1, 1), halves, 2),
+        (halves, 2),
+        (halves,),
+        (halves,),
+        (max(halves - 1, 1),),
+    ]
+    scratch = [pltpu.VMEM(lead + shape, jnp.bfloat16) for lead in leads for shape in shapes]
+    copies = 3 + (pairs - 1) + 2 * (halves - 1)
+    sems = [pltpu.SemaphoreType.DMA((count, copies))] * 2
+    totals = pl.pallas_call(
+        functools.partial(reduce_kernel, count, pairs, halves),
+        out_shape=[jax.ShapeDtypeStruct((halves, 2) + shape, jnp.bfloat16) for shape in shapes],
+        in_specs=[pl.BlockSpec(memory_space=pltpu.VMEM)] * count,
+        out_specs=[pl.BlockSpec(memory_space=pltpu.VMEM)] * count,
+        scratch_shapes=scratch + sems,
+        compiler_params=pltpu.CompilerParams(collective_id=0, has_side_effects=True),
+    )(*blocks)
+    return [
+        total.reshape(grad.shape[0] // owners, grad.shape[1]) for total, grad in zip(totals, grads)
+    ]
 
 
 def shifted_rows(field, size):
@@ -171,15 +329,9 @@
     out_tiles = (middle + mm("wif,fc->wic", act_low, reduce_full)).astype(jnp.bfloat16)
     output = unshifted_rows(from_windows(out_tiles, num_rows, num_cols), size)[None]
 
-    def to_owner(grad):
-        share = lax.psum_scatter(
-            grad.astype(jnp.bfloat16), "fsdp", scatter_dimension=0, tiled=True
-        )
-        return lax.psum(share, "seq")
-
-    reduce_total = to_owner(mm("wif,wic->fc", act_low, cot))
+    reduce_grad = mm("wif,wic->fc", act_low, cot)
     hidden_grad = (mm("wic,fc->wif", cot, reduce_full) * slope).astype(jnp.bfloat16)
-    expand_total = to_owner(mm("wic,wif->cf", second_low, hidden_grad))
+    expand_grad = mm("wic,wif->cf", second_low, hidden_grad)
     upstream_two = mm("wif,cf->wic", hidden_grad, expand_full)
     back_two, gain_two_grad, offset_two_grad = norm_back(upstream_two, hat_two, inv_two, gain_two)
     middle_grad = cot.astype(jnp.float32) + back_two
@@ -212,12 +364,16 @@
         ],
         axis=1,
     )
-    qkv_total = to_owner(qkv_grad_w)
-    proj_total = to_owner(proj_grad)
-    small_total = lax.psum(small_grads, ("fsdp", "seq"))
-    small_total = lax.dynamic_slice_in_dim(small_total, lax.axis_index("fsdp"), 1, 0)[0]
+    step = size * 16 * 128
+    extra = -small_grads.shape[1] % step
+    small_grads = jnp.pad(small_grads, ((0, 0), (0, extra))).reshape(-1, 128)
+    wanted = (expand_grad, reduce_grad, qkv_grad_w, proj_grad, small_grads)
+    expand_total, reduce_total, qkv_total, proj_total, small_total = reduce_all(
+        [grad.astype(jnp.bfloat16) for grad in wanted], owners, size
+    )
+    small_total = small_total.reshape(-1).astype(jnp.float32)
     own = [small_total[at * part : (at + 1) * part] for at in range(4)]
-    table_total = small_total[4 * part :].reshape(table_rows, entries)
+    table_total = small_total[4 * part : 4 * part + table_rows * entries].reshape(table_rows, entries)
     wide = jnp.float32
     return (
         output,

time: 322 us -> 211 us (0.66)
  waiting for transfers between devices: 172 us -> 26.2 us
  Pallas kernels: 0 us -> 79.8 us
  blocking collectives: 59.8 us -> 18.8 us
    reduce_scatter x4 -> x0, waiting for transfers between devices: 99.5 us -> none  [to_owner(): lax.psum_scatter(grad.astype(jnp.bfloat16), 'fsdp', scatter_dimension=0,...]
    pallas_call x0 -> x1, Pallas kernels: none -> 79.8 us  [reduce_all(): pl.pallas_call(functools.partial(reduce_kernel, count, pairs, halves), ou...]
    psum x1 -> x0, waiting for transfers between devices: 46.8 us -> none  [to_owner(): return lax.psum(share, 'seq')]
    psum x1 -> x0, blocking collectives: 41 us -> none  [shards(): small_total = lax.psum(small_grads, ('fsdp', 'seq'))]
    unnamed x77 -> x95, local copies, waits for them, and re-layouts: 6.01 us -> 6.58 us
  transfers between devices with their start and end apart: 12 -> 7, of which waited for: 7 -> 2; matrix products, arithmetic and copies ran while one was open for 13% -> 15% of each run, Pallas kernels for 0% -> 38%
where the time goes in v2:
time: 211 us; the launch traced here: 210 us
  Pallas kernels  79.8 us (38%)
  matrix products  29 us (14%)
  waiting for transfers between devices  26.2 us (12%)
  local copies, waits for them, and re-layouts  22 us (10%)
  blocking collectives  18.8 us (9%)
  between operations  15.2 us (7%)
  starting transfers between devices  9.82 us (5%)
  other arithmetic  9.07 us (4%)
    pallas_call x1, Pallas kernels, reduce_all(): pl.pallas_call(functools.partial(reduce_kernel, count, pairs, halves), ou...  79.8 us
    dot_general x17, matrix products, mm(): return jnp.einsum(form, left, right, preferred_element_type=jnp.float32)  25.1 us
    all_gather x1, waiting for transfers between devices, shards(): reduce_full = lax.all_gather(reduce_weight, 'fsdp', axis=0, tiled=True)  20.2 us
    unnamed x1, blocking collectives  11.7 us
    all_gather x1, blocking collectives, shards(): proj_full = lax.all_gather(proj_weight, 'fsdp', axis=0, tiled=True)  7.07 us
    ppermute x2, starting transfers between devices, shifted_rows(): later = lax.ppermute(field[:SHIFT], 'seq', ring)  6.64 us
    unnamed x95, local copies, waits for them, and re-layouts  6.58 us
    all_gather x1, waiting for transfers between devices, shards(): expand_full = lax.all_gather(expand_weight, 'fsdp', axis=0, tiled=True)  4.6 us
  transfers between devices with their start and end apart: 7, of which 2 were waited for; matrix products, arithmetic and copies ran while one was open for 15% of the time, Pallas kernels for 38%

profile of v2, /device:TPU:0, one launch (start us, length us, event | category | flops | bytes accessed | tf_op | source)
XLA Modules:
  0.0 209.7 jit_solution(17586764952634148952)
XLA Ops:
  8.8 0.9 slice.125
  9.8 6.1 %collective-permute-start.2 = (bf16[3,28,512]{2,0,1:T(4,128)(2,1)S(1)}, bf16[3,28,512]{2,0,1:T(4,128)(2,1)S(1)}, u32[]{:S(2)}, u32[]{:S(2)}) collective-permute-start(bf16[3,28,512]{2,0,1:T(4,128)(2,1)S(1)} %bitcast.219), channel_id=1, source_target_pairs={{0,7},{1,0},{2,1},{3,2},{4,3},{5,4},{6,5},{7,6},{8,15},{9,8},{10,9... | collective-permute-start | bytes 258056 | tf_op jit(solution)/shard_map/ppermute | solution.py:249
  20.2 11.7 %all-reduce.1 = bf16[4752]{0:T(1024)(128)(2,1)S(1)} all-reduce(bf16[4752]{0:T(1024)(128)(2,1)S(1)} %dynamic-update-slice), channel_id=2, replica_groups=mesh['fsdp'=4,'seq'=8] {'fsdp'}, use_global_device_ids=true, to_apply=%add.1 | all-reduce | flops 4752 | bytes 19008
  33.4 7.1 %all_gather.21 = bf16[512,512]{1,0:T(8,128)(2,1)S(1)} all-gather(bf16[128,512]{1,0:T(8,128)(2,1)S(1)} %copy-done.24), channel_id=1, replica_groups=mesh['fsdp'=4,'seq'=8] {'fsdp'}, dimensions={0}, use_global_device_ids=true | all-gather | bytes 655360 | tf_op jit(solution)/shard_map/all_gather | solution.py:291
  40.7 1.0 copy.91
  44.0 2.2 %fusion.3 = bf16[4,49,1536]{2,1,0:T(8,128)(2,1)S(1)} fusion(bf16[512,1536]{1,0:T(8,128)(2,1)} %all-gather.5.cloned.1.call-done, f32[1536]{0:T(1024)S(1)} %copy-done.37, f32[4,49,512]{2,0,1:T(4,128)S(1)} %bitcast.183, f32[512]{0:T(512)S(1)} %get-tuple-element.62, f32[512]{0:T(512)S(1)} %get-tuple-element.63, f32[4,49]{1,0:T(4,128)S(1)} %rsqrt.20, ...), kind=kOutput, calls=%fused_computation.10 | convolution fusion | flops 309385216 | bytes 2588192 | tf_op jit(solution)/shard_map/wic,cd->wid/dot_general | solution.py:90
  46.9 1.0 copy.136
  47.9 2.0 fusion.32
  51.8 4.6 %all-gather.7.cloned.1.call-done = bf16[512,2048]{1,0:T(8,128)(2,1)} async-done(((bf16[128,2048]{1,0:T(8,128)(2,1)}), bf16[512,2048]{1,0:T(8,128)(2,1)}) %all-gather.7.cloned.1.call-update) | async-done | bytes 2097168 | tf_op jit(solution)/shard_map/all_gather | solution.py:292
  56.4 4.0 %multiply_convert_fusion = (bf16[4,49,2048]{2,1,0:T(8,128)(2,1)}, f32[4,49,2048]{2,1,0:T(8,128)}) fusion(bf16[512,2048]{1,0:T(8,128)(2,1)} %all-gather.7.cloned.1.call-done, f32[4,49,512]{2,1,0:T(8,128)S(1)} %get-tuple-element.65, f32[512]{0:T(512)S(1)} %get-tuple-element.61, f32[512]{0:T(512)S(1)} %get-tuple-element.60, f32[4,49]{1,0:T(4,128)S(1)} %add_rsqrt_fusion.1, ...), kind=kOutput, calls=%fused_computation.25 | convolution fusion | flops 413550592 | bytes 4912672 | tf_op jit(solution)/shard_map/wic,cf->wif/dot_general | solution.py:90
  60.4 20.2 %all-gather.9.cloned.1.call-done = bf16[2048,512]{1,0:T(8,128)(2,1)} async-done(((bf16[512,512]{1,0:T(8,128)(2,1)}), bf16[2048,512]{1,0:T(8,128)(2,1)}) %all-gather.9.cloned.1.call-update) | async-done | bytes 2097168 | tf_op jit(solution)/shard_map/all_gather | solution.py:293
  80.6 3.3 %fusion.4 = bf16[4,49,2048]{2,1,0:T(8,128)(2,1)S(1)} fusion(bf16[2048,512]{1,0:T(8,128)(2,1)} %all-gather.9.cloned.1.call-done, f32[4,49,2048]{2,1,0:T(8,128)} %get-tuple-element.67, bf16[4,49,512]{2,0,1:T(4,128)(2,1)S(1)} %bitcast.213), kind=kOutput, calls=%fused_computation.11 | convolution fusion | flops 415055872 | bytes 4706304 | tf_op jit(solution)/shard_map/wic,fc->wif/dot_general | solution.py:90
  83.9 1.0 multiply_reduce_fusion.1
  85.9 1.2 fusion.22
  88.6 2.2 %bitcast_convert_fusion.1 = bf16[512,2048]{1,0:T(8,128)(2,1)} fusion(bf16[4,49,2048]{2,1,0:T(8,128)(2,1)S(1)} %fusion.4, f32[4,49,512]{2,1,0:T(8,128)S(1)} %get-tuple-element.65, f32[512]{0:T(512)S(1)} %get-tuple-element.61, f32[512]{0:T(512)S(1)} %get-tuple-element.60, f32[4,49]{1,0:T(4,128)S(1)} %add_rsqrt_fusion.1, f32[4,49]{1,0:T(4,128)S(1)} %broadcast_multiply_fusion.5), kind=kOutput, calls=%fused_computation.1 | convolution fusion | flops 412592128 | bytes 3307040 | tf_op jit(solution)/shard_map/wic,wif->cf/dot_general | solution.py:90
  90.9 1.3 reshape.246
  92.2 2.1 %copy.107 = bf16[4,16,49,32]{2,3,1,0:T(8,128)(2,1)S(1)} copy(bf16[4,16,49,32]{3,1,0,2:T(8,128)(2,1)} %bitcast.191) | data formatting | bytes 401408 | tf_op jit(solution)/shard_map/transpose | solution.py:81
  94.3 1.4 convolution_convert_fusion
  96.4 1.2 fusion.33
  99.9 2.2 %multiply_reduce_fusion.2 = (bf16[512]{0:T(512)(128)(2,1)S(1)}, f32[4,49]{1,0:T(4,128)S(1)}, f32[4,49]{1,0:T(4,128)S(1)}, bf16[512]{0:T(512)(128)(2,1)S(1)}, f32[4,49,512]{2,1,0:T(8,128)S(1)}) fusion(f32[4,49,512]{2,0,1:T(4,128)S(1)} %bitcast.185, f32[4,49]{1,0:T(4,128)S(1)} %rsqrt.20, f32[4,49]{1,0:T(4,128)S(1)} %div.35, f32[512]{0:T(512)S(1)} %copy-done.26, ...), kind=kOutput, calls=%fused_computation.64 | convolution fusion | flops 310989440 | bytes 2985024 | tf_op jit(solution)/shard_map/wid,cd->wic/dot_general | solution.py:90
  103.1 2.0 fusion
  105.1 2.1 bitcast_convert_fusion
  107.2 1.5 collective-permute-start.1
  109.1 1.1 fusion.30
  111.1 1.5 collective-permute-start.3
  112.6 79.8 %shard_map.212 = (bf16[4,2,16,2048]{3,2,1,0:T(8,128)(2,1)}, bf16[4,2,64,512]{3,2,1,0:T(8,128)(2,1)}, bf16[4,2,16,1536]{3,2,1,0:T(8,128)(2,1)}, bf16[4,2,16,512]{3,2,1,0:T(8,128)(2,1)}, bf16[4,2,16,128]{3,2,1,0:T(8,128)(2,1)}) custom-call(bf16[2,2,4,2,16,2048]{5,4,3,2,1,0:T(8,128)(2,1)} %bitcast.192, bf16[2,2,4,2,64,512]{5,4,3,2,1,0:T(8,128)(2,1)} %bitcast.193, ...), custom_call_target="tpu_custom_call" | custom-call | tf_op jit(solution)/shard_map/pallas_call | solution.py:234
  192.4 1.7 bitcast_convert_fusion.5
  194.2 2.0 bitcast_convert_fusion.4
  196.1 1.1 bitcast_convert_fusion.3
  197.2 1.1 bitcast_convert_fusion.2
  198.4 1.3 fusion.62
  202.1 1.2 copy.121
  (179 shorter events, 21.6 us)
Async XLA Ops:
  7.2 25.0 %copy-start = (s32[56,28]{0,1:T(8,128)S(1)}, s32[56,28]{0,1:T(8,128)}, u32[]{:S(2)}) copy-start(s32[56,28]{0,1:T(8,128)} %param.15) | copy-start | bytes 18820
  7.2 10.4 %copy-start.36 = (u32[32]{0:T(128)S(1)}, u32[32]{0:T(128)}, u32[]{:S(2)}) copy-start(u32[32]{0:T(128)} %constant.50) | copy-start | bytes 388
  7.2 10.3 %copy-start.27 = (bf16[4,169]{1,0:T(4,128)(2,1)S(1)}, bf16[4,169]{1,0:T(4,128)(2,1)}, u32[]{:S(2)}) copy-start(bf16[4,169]{1,0:T(4,128)(2,1)} %param.21) | copy-start | bytes 4060
  7.2 11.6 %copy-start.30 = (bf16[128]{0:T(256)(128)(2,1)S(1)}, bf16[128]{0:T(256)(128)(2,1)}, u32[]{:S(2)}) copy-start(bf16[128]{0:T(256)(128)(2,1)} %param.17) | copy-start | bytes 772
  7.2 11.9 %copy-start.31 = (bf16[128]{0:T(256)(128)(2,1)S(1)}, bf16[128]{0:T(256)(128)(2,1)}, u32[]{:S(2)}) copy-start(bf16[128]{0:T(256)(128)(2,1)} %param.18) | copy-start | bytes 772
  7.2 12.1 %copy-start.32 = (bf16[128]{0:T(256)(128)(2,1)S(1)}, bf16[128]{0:T(256)(128)(2,1)}, u32[]{:S(2)}) copy-start(bf16[128]{0:T(256)(128)(2,1)} %param.22) | copy-start | bytes 772
  7.2 12.3 %copy-start.33 = (bf16[128]{0:T(256)(128)(2,1)S(1)}, bf16[128]{0:T(256)(128)(2,1)}, u32[]{:S(2)}) copy-start(bf16[128]{0:T(256)(128)(2,1)} %param.23) | copy-start | bytes 772
  7.3 25.3 %copy-start.34 = (s32[49,49]{1,0:T(8,128)S(1)}, s32[49,49]{1,0:T(8,128)}, u32[]{:S(2)}) copy-start(s32[49,49]{1,0:T(8,128)} %param.16) | copy-start | bytes 28816
  7.3 26.1 %copy-start.24 = (bf16[128,512]{1,0:T(8,128)(2,1)S(1)}, bf16[128,512]{1,0:T(8,128)(2,1)}, u32[]{:S(2)}) copy-start(bf16[128,512]{1,0:T(8,128)(2,1)} %param.20) | copy-start | bytes 393220
  7.3 36.7 %all-gather.5.cloned.1.call-start = ((), (), s32[]{:S(2)}) async-start(), calls=%async_computation | async-start | bytes 1966080 | tf_op jit(solution)/shard_map/all_gather | solution.py:290
  8.0 48.4 %all-gather.7.cloned.1.call-start = ((), (), s32[]{:S(2)}) async-start(), calls=%async_computation.1 | async-start | bytes 2621440 | tf_op jit(solution)/shard_map/all_gather | solution.py:292
  8.8 71.8 %all-gather.9.cloned.1.call-start = ((), (), s32[]{:S(2)}) async-start(), calls=%async_computation.2 | async-start | bytes 2621440 | tf_op jit(solution)/shard_map/all_gather | solution.py:293
  9.7 30.7 %slice-start.1 = ((bf16[1,7,28,512]{3,2,1,0:T(8,128)(2,1)}), bf16[1,4,28,512]{3,2,1,0:T(8,128)(2,1)S(1)}, s32[]{:S(2)}) async-start(bf16[1,7,28,512]{3,2,1,0:T(8,128)(2,1)} %param.13), calls=%async_computation.4 | async-start | bytes 262144 | tf_op jit(solution)/shard_map/slice | solution.py:250
  9.8 30.8 %slice-start = ((bf16[1,7,28,512]{3,2,1,0:T(8,128)(2,1)}), bf16[1,4,28,512]{3,2,1,0:T(8,128)(2,1)S(1)}, s32[]{:S(2)}) async-start(bf16[1,7,28,512]{3,2,1,0:T(8,128)(2,1)} %param.14), calls=%async_computation.3 | async-start | bytes 262144 | tf_op jit(solution)/shard_map/slice | solution.py:250
  9.8 31.9 %collective-permute-start.2 = (bf16[3,28,512]{2,0,1:T(4,128)(2,1)S(1)}, bf16[3,28,512]{2,0,1:T(4,128)(2,1)S(1)}, u32[]{:S(2)}, u32[]{:S(2)}) collective-permute-start(bf16[3,28,512]{2,0,1:T(4,128)(2,1)S(1)} %bitcast.219), channel_id=1, source_target_pairs={{0,7},{1,0},{2,1},{3,2},{4,3},{5,4},{6,5},{7,6},{8,15},{9,8},{10,9... | collective-permute-start | bytes 258056 | tf_op jit(solution)/shard_map/ppermute | solution.py:249
  16.9 25.8 %collective-permute-start = (bf16[3,28,512]{2,0,1:T(4,128)(2,1)S(1)}, bf16[3,28,512]{2,0,1:T(4,128)(2,1)S(1)}, u32[]{:S(2)}, u32[]{:S(2)}) collective-permute-start(bf16[3,28,512]{2,0,1:T(4,128)(2,1)S(1)} %bitcast.218), channel_id=1, source_target_pairs={{0,7},{1,0},{2,1},{3,2},{4,3},{5,4},{6,5},{7,6},{8,15},{9,8},{10,9... | collective-permute-start | bytes 258056 | tf_op jit(solution)/shard_map/ppermute | solution.py:249
  32.0 11.9 %copy-start.25 = (f32[512]{0:T(512)}, f32[512]{0:T(512)S(1)}, u32[]{:S(2)}) copy-start(f32[512]{0:T(512)S(1)} %get-tuple-element.63) | copy-start | bytes 6148
  32.0 11.9 %copy-start.28 = (f32[512]{0:T(512)}, f32[512]{0:T(512)S(1)}, u32[]{:S(2)}) copy-start(f32[512]{0:T(512)S(1)} %get-tuple-element.62) | copy-start | bytes 6148
  43.9 2.3 %copy-start.5 = (f32[1,4,7,7,512]{4,1,3,2,0:T(4,128)}, f32[1,4,7,7,512]{4,1,3,2,0:T(4,128)S(1)}, u32[]{:S(2)}) copy-start(f32[1,4,7,7,512]{4,1,3,2,0:T(4,128)S(1)} %copy.83) | copy-start | bytes 1204228
  46.5 3.4 %copy-start.12 = (bf16[4,49,512]{1,2,0:T(8,128)(2,1)}, bf16[4,49,512]{1,2,0:T(8,128)(2,1)S(1)}, u32[]{:S(2)}) copy-start(bf16[4,49,512]{1,2,0:T(8,128)(2,1)S(1)} %copy.135) | copy-start | bytes 602116
  46.9 3.1 %copy-start.3 = (bf16[4,49,512]{1,2,0:T(8,128)(2,1)}, bf16[4,49,512]{1,2,0:T(8,128)(2,1)S(1)}, u32[]{:S(2)}) copy-start(bf16[4,49,512]{1,2,0:T(8,128)(2,1)S(1)} %copy.134) | copy-start | bytes 602116
  56.4 24.2 %copy-start.18 = (bf16[1,4,7,7,512]{4,1,3,2,0:T(4,128)(2,1)S(1)}, bf16[1,4,7,7,512]{4,1,3,2,0:T(4,128)(2,1)}, u32[]{:S(2)}) copy-start(bf16[1,4,7,7,512]{4,1,3,2,0:T(4,128)(2,1)} %copy.103) | copy-start | bytes 602116
  80.6 3.3 %copy-start.11 = (bf16[512,2048]{1,0:T(8,128)(2,1)S(1)}, bf16[512,2048]{1,0:T(8,128)(2,1)}, u32[]{:S(2)}) copy-start(bf16[512,2048]{1,0:T(8,128)(2,1)} %all-gather.7.cloned.1.call-done) | copy-start | bytes 6291460
  84.9 2.2 %copy-start.8 = (bf16[4,49,2048]{2,1,0:T(8,128)(2,1)S(1)}, bf16[4,49,2048]{2,1,0:T(8,128)(2,1)}, u32[]{:S(2)}) copy-start(bf16[4,49,2048]{2,1,0:T(8,128)(2,1)} %get-tuple-element.66) | copy-start | bytes 2408452
  92.2 3.5 %copy-start.4 = (bf16[4,49,512]{1,2,0:T(8,128)(2,1)S(1)}, bf16[4,49,512]{1,2,0:T(8,128)(2,1)}, u32[]{:S(2)}) copy-start(bf16[4,49,512]{1,2,0:T(8,128)(2,1)} %copy-done.3) | copy-start | bytes 602116
  99.6 2.5 %copy-start.22 = (bf16[4,49,512]{2,1,0:T(8,128)(2,1)}, bf16[4,49,512]{2,1,0:T(8,128)(2,1)S(1)}, u32[]{:S(2)}) copy-start(bf16[4,49,512]{2,1,0:T(8,128)(2,1)S(1)} %copy.112) | copy-start | bytes 602116
  105.0 3.7 %copy-start.17 = (f32[16,49,49]{1,2,0:T(8,128)S(1)}, f32[16,49,49]{1,2,0:T(8,128)}, u32[]{:S(2)}) copy-start(f32[16,49,49]{1,2,0:T(8,128)} %get-tuple-element.51) | copy-start | bytes 460996
  105.0 4.0 %copy-start.35 = (s32[49,49]{1,0:T(8,128)S(1)}, s32[49,49]{1,0:T(8,128)}, u32[]{:S(2)}) copy-start(s32[49,49]{1,0:T(8,128)} %param.16) | copy-start | bytes 28816
  107.2 93.8 %collective-permute-start.1 = (bf16[3,28,512]{2,0,1:T(4,128)(2,1)S(1)}, bf16[3,28,512]{2,0,1:T(4,128)(2,1)S(1)}, u32[]{:S(2)}, u32[]{:S(2)}) collective-permute-start(bf16[3,28,512]{2,0,1:T(4,128)(2,1)S(1)} %fusion.52), channel_id=1, source_target_pairs={{0,1},{1,2},{2,3},{3,4},{4,5},{5,6},{6,7},{7,0},{8,9},{9,10},{10,1... | collective-permute-start | bytes 258056 | tf_op jit(solution)/shard_map/ppermute | solution.py:257
  111.1 90.8 %collective-permute-start.3 = (f32[3,28,512]{2,0,1:T(4,128)S(1)}, f32[3,28,512]{2,0,1:T(4,128)S(1)}, u32[]{:S(2)}, u32[]{:S(2)}) collective-permute-start(f32[3,28,512]{2,0,1:T(4,128)S(1)} %fusion.43), channel_id=1, source_target_pairs={{0,1},{1,2},{2,3},{3,4},{4,5},{5,6},{6,7},{7,0},{8,9},{9,10},{10,1... | collective-permute-start | bytes 516104 | tf_op jit(solution)/shard_map/ppermute | solution.py:257
  192.4 3.7 %copy-start.21 = (bf16[4,2,16,2048]{3,2,1,0:T(8,128)(2,1)S(1)}, bf16[4,2,16,2048]{3,2,1,0:T(8,128)(2,1)}, u32[]{:S(2)}) copy-start(bf16[4,2,16,2048]{3,2,1,0:T(8,128)(2,1)} %get-tuple-element.19) | copy-start | bytes 1572868
  192.4 4.8 %copy-start.20 = (bf16[4,2,64,512]{3,2,1,0:T(8,128)(2,1)S(1)}, bf16[4,2,64,512]{3,2,1,0:T(8,128)(2,1)}, u32[]{:S(2)}) copy-start(bf16[4,2,64,512]{3,2,1,0:T(8,128)(2,1)} %get-tuple-element.20) | copy-start | bytes 1572868
  (15 other events, 21.3 us)
Sparse Core Ops, SparseCore 0:
  9.6 22.5 all-gather.4
  33.8 22.5 all-gather.6
  58.0 22.5 all-gather.8

commit v3 on v2

--- a/solution.py
+++ b/solution.py
@@ -90,9 +90,12 @@
     return jnp.einsum(form, left, right, preferred_element_type=jnp.float32)
 
 
-def reduce_kernel(count, pairs, halves, *refs):
-    grads, outs = refs[:count], refs[count : 2 * count]
-    rest = refs[2 * count :]
+def reduce_kernel(sources, chunks, pairs, halves, *refs):
+    count = len(chunks)
+    columns = [pl.ds(start, width) for _, start, width in chunks]
+    grads = [refs[at] for at, _, _ in chunks]
+    outs = [refs[sources + at] for at, _, _ in chunks]
+    rest = refs[2 * sources :]
     stages = [rest[at * count : (at + 1) * count] for at in range(7)]
     first_in, first_sum, second_in, second_sum, third_in, third_sum, fourth_in = stages
     send_sem, recv_sem = rest[7 * count :]
@@ -146,7 +149,7 @@
     def sum_pair(at, pair_at):
         @pl.loop(0, 2 * halves)
         def _(piece):
-            mine = grads[at][pair_at, core, piece // 2, piece % 2]
+            mine = grads[at][pair_at, core, piece // 2, piece % 2, :, columns[at]]
             came = first_in[at][pair_at, piece // 2, piece % 2]
             add(first_sum[at], [mine, came], (pair_at, piece // 2, piece % 2))
 
@@ -158,7 +161,7 @@
             add(second_sum[at], terms, (piece, side_at))
 
     def stage_first(at):
-        send(0, at, grads[at].at[:, 1 - core], first_in[at], on_fsdp(pair, 1 - core))
+        send(0, at, grads[at].at[:, 1 - core, :, :, :, columns[at]], first_in[at], on_fsdp(pair, 1 - core))
 
     def stage_second(at):
         arrived(0, at)
@@ -186,14 +189,14 @@
     def stage_fifth(at):
         arrived(3, at)
         terms = [third_sum[at][half]] + [fourth_in[at][step] for step in range(halves - 1)]
-        add(outs[at], terms, (half, side))
-        own = outs[at].at[half, side]
+        add(outs[at], terms, (half, side, slice(None), columns[at]))
+        own = outs[at].at[half, side, :, columns[at]]
         for peer in half_peers:
             send(4, at, own, own, on_seq(peer, side))
 
     def stage_sixth(at):
         arrived(4, at)
-        own = outs[at].at[:, side]
+        own = outs[at].at[:, side, :, columns[at]]
         send(5, at, own, own, on_seq(half, 1 - side))
 
     for at in range(count):
@@ -228,11 +231,19 @@
         (halves,),
         (max(halves - 1, 1),),
     ]
-    scratch = [pltpu.VMEM(lead + shape, jnp.bfloat16) for lead in leads for shape in shapes]
+    chunks = []
+    for at, (rows, columns) in enumerate(shapes):
+        parts = 2 if columns % 256 == 0 and grads[at].size > 2 * grads[-2].size else 1
+        chunks += [(at, step * (columns // parts), columns // parts) for step in range(parts)]
+    scratch = [
+        pltpu.VMEM(lead + (shapes[at][0], width), jnp.bfloat16)
+        for lead in leads
+        for at, _, width in chunks
+    ]
     copies = 3 + (pairs - 1) + 2 * (halves - 1)
-    sems = [pltpu.SemaphoreType.DMA((count, copies))] * 2
+    sems = [pltpu.SemaphoreType.DMA((len(chunks), copies))] * 2
     totals = pl.pallas_call(
-        functools.partial(reduce_kernel, count, pairs, halves),
+        functools.partial(reduce_kernel, count, tuple(chunks), pairs, halves),
         out_shape=[jax.ShapeDtypeStruct((halves, 2) + shape, jnp.bfloat16) for shape in shapes],
         in_specs=[pl.BlockSpec(memory_space=pltpu.VMEM)] * count,
         out_specs=[pl.BlockSpec(memory_space=pltpu.VMEM)] * count,
@@ -242,6 +253,85 @@
     return [
         total.reshape(grad.shape[0] // owners, grad.shape[1]) for total, grad in zip(totals, grads)
     ]
+
+
+def gather_kernel(count, pairs, *refs):
+    shards_in, fulls = refs[:count], refs[count : 2 * count]
+    send_sem, recv_sem, copy_sem = refs[2 * count :]
+    place, line = lax.axis_index("fsdp"), lax.axis_index("seq")
+    pair, core = place // 2, place % 2
+    half, side = line // 2, line % 2
+    mesh_id = pl.DeviceIdType.MESH
+    partner = {"fsdp": pair * 2 + 1 - core, "seq": line}
+    beside = {"fsdp": place, "seq": half * 2 + 1 - side}
+    peers = [(pair + step) % pairs for step in range(1, pairs)]
+    sources = [(pair + pairs - step) % pairs for step in range(1, pairs)]
+    across = [{"fsdp": peer * 2 + core, "seq": line} for peer in peers]
+    barrier = pltpu.get_barrier_semaphore()
+    for device in [partner, beside] + across:
+        pl.semaphore_signal(barrier, inc=1, device_id=device, device_id_type=mesh_id)
+    pl.semaphore_wait(barrier, 2 + len(across))
+
+    started = []
+
+    def send(at, slot, source, target, device):
+        copy = pltpu.make_async_remote_copy(
+            src_ref=source,
+            dst_ref=target,
+            send_sem=send_sem.at[at, slot],
+            recv_sem=recv_sem.at[at, slot],
+            device_id=device,
+            device_id_type=mesh_id,
+        )
+        copy.start()
+        started.append(copy)
+        return copy
+
+    far, near, last, kept = {}, {}, [], []
+    for at in range(count):
+        mine = fulls[at].at[pair, core]
+        for step, device in enumerate(across):
+            target = fulls[at].at[pair, core, side]
+            far[at, step] = send(at, 1 + 3 * step, shards_in[at].at[side], target, device)
+        last.append(send(at, 0, shards_in[at], mine, partner))
+        copy = pltpu.make_async_copy(shards_in[at], mine, copy_sem.at[at])
+        copy.start()
+        kept.append(copy)
+    for tick in range(count + 1):
+        if tick < count:
+            for step, source in enumerate(sources):
+                far[tick, step].wait_recv()
+                came = fulls[tick].at[source, core, side]
+                near[tick, step] = send(tick, 2 + 3 * step, came, came, beside)
+        if tick:
+            for step, source in enumerate(sources):
+                near[tick - 1, step].wait_recv()
+                came = fulls[tick - 1].at[source, core]
+                last.append(send(tick - 1, 3 + 3 * step, came, came, partner))
+    for copy in last:
+        copy.wait_recv()
+    for copy in kept:
+        copy.wait()
+    for copy in started:
+        copy.wait_send()
+
+
+def gather_all(weights, owners):
+    pairs, count = owners // 2, len(weights)
+    shards_in = [weight.reshape(2, weight.shape[0] // 2, weight.shape[1]) for weight in weights]
+    copies = 1 + 3 * (pairs - 1)
+    fulls = pl.pallas_call(
+        functools.partial(gather_kernel, count, pairs),
+        out_shape=[
+            jax.ShapeDtypeStruct((pairs, 2) + shard.shape, shard.dtype) for shard in shards_in
+        ],
+        in_specs=[pl.BlockSpec(memory_space=pltpu.VMEM)] * count,
+        out_specs=[pl.BlockSpec(memory_space=pltpu.VMEM)] * count,
+        scratch_shapes=[pltpu.SemaphoreType.DMA((count, copies))] * 2
+        + [pltpu.SemaphoreType.DMA((count,))],
+        compiler_params=pltpu.CompilerParams(collective_id=1, has_side_effects=True),
+    )(*shards_in)
+    return [full.reshape(-1, full.shape[-1]) for full in fulls]
 
 
 def shifted_rows(field, size):
@@ -279,7 +369,11 @@
     small = jnp.concatenate(
         [first_gain, first_offset, second_gain, second_offset, bias_table.reshape(-1)]
     )
-    small_full = lax.all_gather(small, "fsdp", axis=0, tiled=False)
+    filled = jnp.pad(small, (0, -small.shape[0] % (32 * 128))).reshape(-1, 128)
+    small_full, qkv_full, proj_full, expand_full, reduce_full = gather_all(
+        [filled, qkv_weight, proj_weight, expand_weight, reduce_weight], owners
+    )
+    small_full = small_full.reshape(owners, -1)[:, : small.shape[0]]
     vectors = [
         small_full[:, at * part : (at + 1) * part].reshape(-1).astype(jnp.float32)
         for at in range(4)
@@ -287,10 +381,6 @@
     gain_one, offset_one, gain_two, offset_two = vectors
     table_rows, entries = bias_table.shape
     table_full = small_full[:, 4 * part :].reshape(-1, entries)
-    qkv_full = lax.all_gather(qkv_weight, "fsdp", axis=0, tiled=True)
-    proj_full = lax.all_gather(proj_weight, "fsdp", axis=0, tiled=True)
-    expand_full = lax.all_gather(expand_weight, "fsdp", axis=0, tiled=True)
-    reduce_full = lax.all_gather(reduce_weight, "fsdp", axis=0, tiled=True)
     _, num_rows, num_cols, width = tokens.shape
     num_heads = table_full.shape[0]
     query_scale = (width // num_heads) ** (-0.5)

time: 211 us -> 170 us (0.81)
  waiting for transfers between devices: 26.2 us -> 0.01 us
  Pallas kernels: 79.8 us -> 103 us
  blocking collectives: 18.8 us -> 0 us
  between operations: 15.2 us -> 1.23 us
  matrix products: 29 us -> 22.4 us
  local copies, waits for them, and re-layouts: 22 us -> 25.5 us
  starting transfers between devices: 9.82 us -> 7.46 us
    all_gather x3 -> x0, waiting for transfers between devices: 24.8 us -> none  [the longest x1 20.2 us: shards(): reduce_full = lax.all_gather(reduce_weight, 'fsdp', axis=0, tiled=True)]
    pallas_call x1 -> x2, Pallas kernels: 79.8 us -> 103 us  [the longest x1 70.1 us: reduce_all(): pl.pallas_call(functools.partial(reduce_kernel, count, tuple(chunks), pai...]
    unnamed x1 -> x0, blocking collectives: 11.7 us -> none
    all_gather x1 -> x0, blocking collectives: 7.07 us -> none  [shards(): proj_full = lax.all_gather(proj_weight, 'fsdp', axis=0, tiled=True)]
    dot_general x17, matrix products: 25.1 us -> 18.5 us  [mm(): return jnp.einsum(form, left, right, preferred_element_type=jnp.float32)]
    ppermute x2, starting transfers between devices: 3.06 us -> 0.82 us  [unshifted_rows(): earlier = lax.ppermute(field[keep:], 'seq', ring)]
    unnamed x95 -> x62, local copies, waits for them, and re-layouts: 6.58 us -> 8.74 us
  transfers between devices with their start and end apart: 7 -> 4, of which waited for: 2 -> 0; matrix products, arithmetic and copies ran while one was open for 15% -> 13% of each run, Pallas kernels for 38% -> 61%
where the time goes in v3:
time: 170 us
  Pallas kernels  103 us (61%)
  local copies, waits for them, and re-layouts  25.5 us (15%)
  matrix products  22.4 us (13%)
  other arithmetic  9.82 us (6%)
  starting transfers between devices  7.46 us (4%)
    pallas_call x1, Pallas kernels, reduce_all(): pl.pallas_call(functools.partial(reduce_kernel, count, tuple(chunks), pai...  70.1 us
    pallas_call x1, Pallas kernels, gather_all(): pl.pallas_call(functools.partial(gather_kernel, count, pairs), out_shape=...  33.1 us
    dot_general x17, matrix products, mm(): return jnp.einsum(form, left, right, preferred_element_type=jnp.float32)  18.5 us
    unnamed x62, local copies, waits for them, and re-layouts  8.74 us
    ppermute x2, starting transfers between devices, shifted_rows(): later = lax.ppermute(field[:SHIFT], 'seq', ring)  6.64 us
  transfers between devices with their start and end apart: 4, of which 0 were waited for; matrix products, arithmetic and copies ran while one was open for 13% of the time, Pallas kernels for 61%

profile of v3, /device:TPU:0, one launch (start us, length us, event | category | flops | bytes accessed | tf_op | source)
XLA Modules:
  0.0 169.7 jit_solution(5597691378040561241)
XLA Ops:
  0.7 0.9 slice.131
  1.7 6.1 %collective-permute-start.2 = (bf16[3,28,512]{2,0,1:T(4,128)(2,1)S(1)}, bf16[3,28,512]{2,0,1:T(4,128)(2,1)S(1)}, u32[]{:S(2)}, u32[]{:S(2)}) collective-permute-start(bf16[3,28,512]{2,0,1:T(4,128)(2,1)S(1)} %bitcast.228), channel_id=1, source_target_pairs={{0,7},{1,0},{2,1},{3,2},{4,3},{5,4},{6,5},{7,6},{8,15},{9,8},{10,9... | collective-permute-start | bytes 258056 | tf_op jit(solution)/shard_map/ppermute | solution.py:339
  7.7 0.9 slice.113
  11.2 0.8 dynamic-update-slice.5
  12.0 0.8 dynamic-update-slice.6
  12.8 0.8 dynamic-update-slice.7
  13.7 0.8 dynamic-update-slice.8
  15.3 33.1 %shard_map.212 = (bf16[2,2,2,16,128]{4,3,2,1,0:T(8,128)(2,1)}, bf16[2,2,2,64,1536]{4,3,2,1,0:T(8,128)(2,1)}, bf16[2,2,2,64,512]{4,3,2,1,0:T(8,128)(2,1)}, bf16[2...) custom-call(bf16[2,16,128]{2,1,0:T(8,128)(2,1)} %bitcast.231, bf16[2,64,1536]{2,1,0:T(8,128)(2,1)} %bitcast.226, ...), custom_call_target="tpu_custom_call" | custom-call | tf_op jit(solution)/shard_map/pallas_call | solution.py:323
  50.3 1.0 copy.93
  54.4 1.0 copy.141
  55.4 2.1 %fusion.17 = f32[4,16,49,49]{2,3,1,0:T(8,128)S(1)} fusion(bf16[4,16,49,32]{2,3,1,0:T(8,128)(2,1)} %bitcast.200, bf16[4,16,49,32]{2,3,1,0:T(8,128)(2,1)S(1)} %bitcast.198, f32[4,49,49]{1,2,0:T(8,128)} %compare_select_fusion, f32[16,49,49]{1,2,0:T(8,128)} %copy.93), kind=kOutput, calls=%fused_computation.37 | convolution fusion | flops 10298672 | bytes 1208144 | tf_op jit(solution)/shard_map/div | solution.py:409
  59.6 0.9 multiply_convert_fusion
  61.2 1.0 fusion.4
  62.2 1.4 multiply_reduce_fusion.1
  64.2 1.2 fusion.12
  66.9 2.2 %bitcast_convert_fusion.1 = bf16[512,2048]{1,0:T(8,128)(2,1)} fusion(bf16[4,49,2048]{2,1,0:T(8,128)(2,1)S(1)} %fusion.4, f32[4,49,512]{2,1,0:T(8,128)S(1)} %get-tuple-element.75, f32[512]{0:T(512)S(1)} %get-tuple-element.71, f32[512]{0:T(512)S(1)} %get-tuple-element.70, f32[4,49]{1,0:T(4,128)S(1)} %add_rsqrt_fusion.1, f32[4,49]{1,0:T(4,128)S(1)} %broadcast_multiply_fusion.5), kind=kOutput, calls=%fused_computation.1 | convolution fusion | flops 412592128 | bytes 3307040 | tf_op jit(solution)/shard_map/wic,wif->cf/dot_general | solution.py:90
  69.2 1.3 reshape.283
  70.5 2.0 %copy.110 = bf16[4,16,49,32]{2,3,1,0:T(8,128)(2,1)S(1)} copy(bf16[4,16,49,32]{3,1,0,2:T(8,128)(2,1)} %bitcast.188) | data formatting | bytes 401408 | tf_op jit(solution)/shard_map/transpose | solution.py:81
  72.5 1.4 convolution_convert_fusion
  73.9 0.9 multiply_reduce_fusion
  74.8 1.2 fusion.18
  78.4 2.2 %multiply_reduce_fusion.2 = (bf16[512]{0:T(512)(128)(2,1)S(1)}, f32[4,49]{1,0:T(4,128)S(1)}, f32[4,49]{1,0:T(4,128)S(1)}, bf16[512]{0:T(512)(128)(2,1)S(1)}, f32[4,49,512]{2,1,0:T(8,128)S(1)}) fusion(f32[4,49,512]{2,0,1:T(4,128)S(1)} %bitcast.185, f32[4,49]{1,0:T(4,128)S(1)} %div.43, f32[4,49]{1,0:T(4,128)S(1)} %rsqrt.22, f32[512]{0:T(512)S(1)} %get-tuple-element.73, ...), kind=kOutput, calls=%fused_computation.52 | convolution fusion | flops 310989440 | bytes 2985024 | tf_op jit(solution)/shard_map/wid,cd->wic/dot_general | solution.py:90
  81.4 1.9 %fusion = bf16[512,1536]{1,0:T(8,128)(2,1)} fusion(bf16[4,49,512]{2,1,0:T(8,128)(2,1)S(1)} %copy.117, bf16[4,49,512]{2,1,0:T(8,128)(2,1)S(1)} %copy.116, bf16[4,49,512]{2,1,0:T(8,128)(2,1)S(1)} %copy.115, f32[4,49,512]{2,0,1:T(4,128)S(1)} %bitcast.187, f32[512]{0:T(512)S(1)} %get-tuple-element.72, f32[4,49]{1,0:T(4,128)S(1)} %div.43, ...), kind=kOutput, calls=%fused_computation.3 | convolution fusion | flops 311375872 | bytes 2582048 | tf_op jit(solution)/shard_map/wic,wid->cd/dot_general | solution.py:90
  83.4 2.0 %bitcast_convert_fusion = bf16[2048,512]{1,0:T(8,128)(2,1)} fusion(bf16[4,49,2048]{2,1,0:T(8,128)(2,1)S(1)} %copy-done.4, bf16[4,49,512]{2,0,1:T(4,128)(2,1)S(1)} %bitcast.221), kind=kOutput, calls=%fused_computation | convolution fusion | flops 412090368 | bytes 3100672 | tf_op jit(solution)/shard_map/wif,wic->fc/dot_general | solution.py:90
  86.6 1.1 fusion.15
  88.7 70.1 %shard_map.213 = (bf16[4,2,16,2048]{3,2,1,0:T(8,128)(2,1)}, bf16[4,2,64,512]{3,2,1,0:T(8,128)(2,1)}, bf16[4,2,16,1536]{3,2,1,0:T(8,128)(2,1)}, bf16[4,2,16,512]{3,2,1,0:T(8,128)(2,1)}, bf16[4,2,16,128]{3,2,1,0:T(8,128)(2,1)}) custom-call(bf16[2,2,4,2,16,2048]{5,4,3,2,1,0:T(8,128)(2,1)} %bitcast.189, bf16[2,2,4,2,64,512]{5,4,3,2,1,0:T(8,128)(2,1)} %bitcast.190, ...), custom_call_target="tpu_custom_call" | custom-call | tf_op jit(solution)/shard_map/pallas_call | solution.py:245
  158.9 1.7 %bitcast_convert_fusion.5 = f32[128,512]{1,0:T(8,128)} fusion(bf16[4,2,16,512]{3,2,1,0:T(8,128)(2,1)} %get-tuple-element.28), kind=kLoop, calls=%fused_computation.93 | loop fusion | flops 65536 | bytes 393216 | tf_op jit(solution)/shard_map/convert_element_type | solution.py:474
  160.6 2.0 %bitcast_convert_fusion.4 = f32[128,1536]{1,0:T(8,128)} fusion(bf16[4,2,16,1536]{3,2,1,0:T(8,128)(2,1)} %get-tuple-element.27), kind=kLoop, calls=%fused_computation.67 | loop fusion | flops 196608 | bytes 1179648 | tf_op jit(solution)/shard_map/convert_element_type | solution.py:473
  162.6 1.1 bitcast_convert_fusion.3
  163.7 1.1 bitcast_convert_fusion.2
  164.8 1.3 fusion.52
  168.5 1.2 copy.126
  (139 shorter events, 20.6 us)
Async XLA Ops:
  0.6 9.4 %copy-start = (s32[56,28]{0,1:T(8,128)S(1)}, s32[56,28]{0,1:T(8,128)}, u32[]{:S(2)}) copy-start(s32[56,28]{0,1:T(8,128)} %param.15) | copy-start | bytes 18820
  0.7 48.6 %copy-start.21 = (s32[49,49]{1,0:T(8,128)S(1)}, s32[49,49]{1,0:T(8,128)}, u32[]{:S(2)}) copy-start(s32[49,49]{1,0:T(8,128)} %param.16) | copy-start | bytes 28816
  1.7 50.3 %collective-permute-start.2 = (bf16[3,28,512]{2,0,1:T(4,128)(2,1)S(1)}, bf16[3,28,512]{2,0,1:T(4,128)(2,1)S(1)}, u32[]{:S(2)}, u32[]{:S(2)}) collective-permute-start(bf16[3,28,512]{2,0,1:T(4,128)(2,1)S(1)} %bitcast.228), channel_id=1, source_target_pairs={{0,7},{1,0},{2,1},{3,2},{4,3},{5,4},{6,5},{7,6},{8,15},{9,8},{10,9... | collective-permute-start | bytes 258056 | tf_op jit(solution)/shard_map/ppermute | solution.py:339
  8.6 41.4 %slice-start.1 = ((bf16[1,7,28,512]{3,2,1,0:T(8,128)(2,1)}), bf16[1,4,28,512]{3,2,1,0:T(8,128)(2,1)S(1)}, s32[]{:S(2)}) async-start(bf16[1,7,28,512]{3,2,1,0:T(8,128)(2,1)} %param.13), calls=%async_computation.1 | async-start | bytes 262144 | tf_op jit(solution)/shard_map/slice | solution.py:340
  8.7 41.4 %slice-start = ((bf16[1,7,28,512]{3,2,1,0:T(8,128)(2,1)}), bf16[1,4,28,512]{3,2,1,0:T(8,128)(2,1)S(1)}, s32[]{:S(2)}) async-start(bf16[1,7,28,512]{3,2,1,0:T(8,128)(2,1)} %param.14), calls=%async_computation | async-start | bytes 262144 | tf_op jit(solution)/shard_map/slice | solution.py:340
  8.7 42.6 %collective-permute-start = (bf16[3,28,512]{2,0,1:T(4,128)(2,1)S(1)}, bf16[3,28,512]{2,0,1:T(4,128)(2,1)S(1)}, u32[]{:S(2)}, u32[]{:S(2)}) collective-permute-start(bf16[3,28,512]{2,0,1:T(4,128)(2,1)S(1)} %bitcast.229), channel_id=1, source_target_pairs={{0,7},{1,0},{2,1},{3,2},{4,3},{5,4},{6,5},{7,6},{8,15},{9,8},{10,9... | collective-permute-start | bytes 258056 | tf_op jit(solution)/shard_map/ppermute | solution.py:339
  51.8 1.4 copy-start.14
  51.8 1.4 copy-start.19
  52.3 11.4 %copy-start.15 = (bf16[1,4,7,7,512]{4,1,3,2,0:T(4,128)(2,1)}, bf16[1,4,7,7,512]{4,1,3,2,0:T(4,128)(2,1)S(1)}, u32[]{:S(2)}) copy-start(bf16[1,4,7,7,512]{4,1,3,2,0:T(4,128)(2,1)S(1)} %copy.105) | copy-start | bytes 602116
  52.7 5.2 %copy-start.1 = (f32[1,4,7,7,512]{4,1,3,2,0:T(4,128)}, f32[1,4,7,7,512]{4,1,3,2,0:T(4,128)S(1)}, u32[]{:S(2)}) copy-start(f32[1,4,7,7,512]{4,1,3,2,0:T(4,128)S(1)} %copy.86) | copy-start | bytes 1204228
  54.1 3.4 %copy-start.8 = (bf16[4,49,512]{1,2,0:T(8,128)(2,1)}, bf16[4,49,512]{1,2,0:T(8,128)(2,1)S(1)}, u32[]{:S(2)}) copy-start(bf16[4,49,512]{1,2,0:T(8,128)(2,1)S(1)} %copy.140) | copy-start | bytes 602116
  57.5 1.0 copy-start.5
  57.9 1.6 copy-start.7
  59.6 1.6 copy-start.6
  60.4 5.0 %copy-start.3 = (bf16[4,49,2048]{2,1,0:T(8,128)(2,1)}, bf16[4,49,2048]{2,1,0:T(8,128)(2,1)S(1)}, u32[]{:S(2)}) copy-start(bf16[4,49,2048]{2,1,0:T(8,128)(2,1)S(1)} %get-tuple-element.76) | copy-start | bytes 2408452
  74.8 1.2 copy-start.10
  76.0 1.0 copy-start.9
  76.0 1.6 copy-start.11
  77.1 1.3 copy-start.2
  81.4 2.0 %copy-start.4 = (bf16[4,49,2048]{2,1,0:T(8,128)(2,1)S(1)}, bf16[4,49,2048]{2,1,0:T(8,128)(2,1)}, u32[]{:S(2)}) copy-start(bf16[4,49,2048]{2,1,0:T(8,128)(2,1)} %copy-done.3) | copy-start | bytes 2408452
  81.4 2.0 %copy-start.16 = (bf16[1,4,7,7,512]{4,1,3,2,0:T(4,128)(2,1)S(1)}, bf16[1,4,7,7,512]{4,1,3,2,0:T(4,128)(2,1)}, u32[]{:S(2)}) copy-start(bf16[1,4,7,7,512]{4,1,3,2,0:T(4,128)(2,1)} %copy-done.15) | copy-start | bytes 602116
  83.4 2.1 %copy-start.12 = (bf16[7,25,512]{2,0,1:T(8,128)(2,1)S(1)}, bf16[7,25,512]{2,0,1:T(8,128)(2,1)}, u32[]{:S(2)}) copy-start(bf16[7,25,512]{2,0,1:T(8,128)(2,1)} %slice.155) | copy-start | bytes 537604
  83.4 2.9 %copy-start.13 = (f32[16,49,49]{1,2,0:T(8,128)S(1)}, f32[16,49,49]{1,2,0:T(8,128)}, u32[]{:S(2)}) copy-start(f32[16,49,49]{1,2,0:T(8,128)} %get-tuple-element.61) | copy-start | bytes 460996
  83.4 3.2 %copy-start.22 = (s32[49,49]{1,0:T(8,128)S(1)}, s32[49,49]{1,0:T(8,128)}, u32[]{:S(2)}) copy-start(s32[49,49]{1,0:T(8,128)} %param.16) | copy-start | bytes 28816
  85.4 2.4 %copy-start.20 = (bf16[512]{0:T(512)(128)(2,1)S(1)}, bf16[512]{0:T(512)(128)(2,1)}, u32[]{:S(2)}) copy-start(bf16[512]{0:T(512)(128)(2,1)} %get-tuple-element.53) | copy-start | bytes 3076
  85.5 82.0 %collective-permute-start.1 = (bf16[3,28,512]{2,0,1:T(4,128)(2,1)S(1)}, bf16[3,28,512]{2,0,1:T(4,128)(2,1)S(1)}, u32[]{:S(2)}, u32[]{:S(2)}) collective-permute-start(bf16[3,28,512]{2,0,1:T(4,128)(2,1)S(1)} %fusion.41), channel_id=1, source_target_pairs={{0,1},{1,2},{2,3},{3,4},{4,5},{5,6},{6,7},{7,0},{8,9},{9,10},{10,1... | collective-permute-start | bytes 258056 | tf_op jit(solution)/shard_map/ppermute | solution.py:347
  88.6 79.8 %collective-permute-start.3 = (f32[3,28,512]{2,0,1:T(4,128)S(1)}, f32[3,28,512]{2,0,1:T(4,128)S(1)}, u32[]{:S(2)}, u32[]{:S(2)}) collective-permute-start(f32[3,28,512]{2,0,1:T(4,128)S(1)} %fusion.27), channel_id=1, source_target_pairs={{0,1},{1,2},{2,3},{3,4},{4,5},{5,6},{6,7},{7,0},{8,9},{9,10},{10,1... | collective-permute-start | bytes 516104 | tf_op jit(solution)/shard_map/ppermute | solution.py:347
  158.9 3.7 %copy-start.18 = (bf16[4,2,16,2048]{3,2,1,0:T(8,128)(2,1)S(1)}, bf16[4,2,16,2048]{3,2,1,0:T(8,128)(2,1)}, u32[]{:S(2)}) copy-start(bf16[4,2,16,2048]{3,2,1,0:T(8,128)(2,1)} %get-tuple-element.29) | copy-start | bytes 1572868
  158.9 4.8 %copy-start.17 = (bf16[4,2,64,512]{3,2,1,0:T(8,128)(2,1)S(1)}, bf16[4,2,64,512]{3,2,1,0:T(8,128)(2,1)}, u32[]{:S(2)}) copy-start(bf16[4,2,64,512]{3,2,1,0:T(8,128)(2,1)} %get-tuple-element.30) | copy-start | bytes 1572868

commit v4 on v3

--- a/solution.py
+++ b/solution.py
@@ -202,10 +202,10 @@
     for at in range(count):
         stage_first(at)
     later = (stage_second, stage_third, stage_fourth, stage_fifth, stage_sixth)
-    for tick in range(count + len(later) - 1):
+    for tick in range(count + 2 * (len(later) - 1)):
         for lag, stage in enumerate(later):
-            if 0 <= tick - lag < count:
-                stage(tick - lag)
+            if 0 <= tick - 2 * lag < count:
+                stage(tick - 2 * lag)
     for at in range(count):
         arrived(5, at)
     for copies in started.values():
@@ -233,7 +233,7 @@
     ]
     chunks = []
     for at, (rows, columns) in enumerate(shapes):
-        parts = 2 if columns % 256 == 0 and grads[at].size > 2 * grads[-2].size else 1
+        parts = 4 if columns % 512 == 0 and grads[at].size > 2 * grads[-2].size else 1
         chunks += [(at, step * (columns // parts), columns // parts) for step in range(parts)]
     scratch = [
         pltpu.VMEM(lead + (shapes[at][0], width), jnp.bfloat16)
@@ -370,8 +370,8 @@
         [first_gain, first_offset, second_gain, second_offset, bias_table.reshape(-1)]
     )
     filled = jnp.pad(small, (0, -small.shape[0] % (32 * 128))).reshape(-1, 128)
-    small_full, qkv_full, proj_full, expand_full, reduce_full = gather_all(
-        [filled, qkv_weight, proj_weight, expand_weight, reduce_weight], owners
+    expand_full, reduce_full, qkv_full, proj_full, small_full = gather_all(
+        [expand_weight, reduce_weight, qkv_weight, proj_weight, filled], owners
     )
     small_full = small_full.reshape(owners, -1)[:, : small.shape[0]]
     vectors = [

time: 170 us -> 168 us (0.988)
  Pallas kernels: 103 us -> 100 us
    pallas_call x1, Pallas kernels: 70.1 us -> 66.2 us  [reduce_all(): pl.pallas_call(functools.partial(reduce_kernel, count, tuple(chunks), pai...]
  transfers between devices with their start and end apart: 4 -> 4, of which waited for: 0 -> 0; matrix products, arithmetic and copies ran while one was open for 13% -> 13% of each run, Pallas kernels for 61% -> 60%
where the time goes in v4:
time: 168 us; the launch traced here: 167 us
  Pallas kernels  100 us (60%)
  local copies, waits for them, and re-layouts  25.5 us (15%)
  matrix products  22.4 us (13%)
  other arithmetic  9.82 us (6%)
  starting transfers between devices  8.16 us (5%)
    pallas_call x1, Pallas kernels, reduce_all(): pl.pallas_call(functools.partial(reduce_kernel, count, tuple(chunks), pai...  66.2 us
    pallas_call x1, Pallas kernels, gather_all(): pl.pallas_call(functools.partial(gather_kernel, count, pairs), out_shape=...  33.8 us
    dot_general x17, matrix products, mm(): return jnp.einsum(form, left, right, preferred_element_type=jnp.float32)  18.5 us
    unnamed x62, local copies, waits for them, and re-layouts  8.74 us
    ppermute x2, starting transfers between devices, shifted_rows(): later = lax.ppermute(field[:SHIFT], 'seq', ring)  6.64 us
  transfers between devices with their start and end apart: 4, of which 0 were waited for; matrix products, arithmetic and copies ran while one was open for 13% of the time, Pallas kernels for 60%

profile of v4, /device:TPU:0, one launch (start us, length us, event | category | flops | bytes accessed | tf_op | source)
XLA Modules:
  0.0 167.2 jit_solution(13336618065937444915)
XLA Ops:
  0.7 0.9 slice.131
  1.7 6.1 %collective-permute-start.2 = (bf16[3,28,512]{2,0,1:T(4,128)(2,1)S(1)}, bf16[3,28,512]{2,0,1:T(4,128)(2,1)S(1)}, u32[]{:S(2)}, u32[]{:S(2)}) collective-permute-start(bf16[3,28,512]{2,0,1:T(4,128)(2,1)S(1)} %bitcast.228), channel_id=1, source_target_pairs={{0,7},{1,0},{2,1},{3,2},{4,3},{5,4},{6,5},{7,6},{8,15},{9,8},{10,9... | collective-permute-start | bytes 258056 | tf_op jit(solution)/shard_map/ppermute | solution.py:339
  7.7 0.9 slice.113
  12.0 0.8 dynamic-update-slice.6
  12.8 0.8 dynamic-update-slice.7
  13.7 0.8 dynamic-update-slice.8
  15.3 33.8 %shard_map.212 = (bf16[2,2,2,64,2048]{4,3,2,1,0:T(8,128)(2,1)}, bf16[2,2,2,256,512]{4,3,2,1,0:T(8,128)(2,1)}, bf16[2,2,2,64,1536]{4,3,2,1,0:T(8,128)(2,1)}, bf16...) custom-call(bf16[2,64,2048]{2,1,0:T(8,128)(2,1)} %bitcast.223, bf16[2,256,512]{2,1,0:T(8,128)(2,1)} %bitcast.224, ...), custom_call_target="tpu_custom_call" | custom-call | tf_op jit(solution)/shard_map/pallas_call | solution.py:323
  51.0 1.0 copy.93
  55.2 1.0 copy.141
  56.2 2.1 %fusion.17 = f32[4,16,49,49]{2,3,1,0:T(8,128)S(1)} fusion(bf16[4,16,49,32]{2,3,1,0:T(8,128)(2,1)} %bitcast.200, bf16[4,16,49,32]{2,3,1,0:T(8,128)(2,1)S(1)} %bitcast.198, f32[4,49,49]{1,2,0:T(8,128)} %compare_select_fusion, f32[16,49,49]{1,2,0:T(8,128)} %copy.93), kind=kOutput, calls=%fused_computation.37 | convolution fusion | flops 10298672 | bytes 1208144 | tf_op jit(solution)/shard_map/div | solution.py:409
  60.3 0.9 multiply_convert_fusion
  61.9 1.0 fusion.4
  63.0 1.4 multiply_reduce_fusion.1
  65.0 1.2 fusion.12
  67.7 2.2 %bitcast_convert_fusion.1 = bf16[512,2048]{1,0:T(8,128)(2,1)} fusion(bf16[4,49,2048]{2,1,0:T(8,128)(2,1)S(1)} %fusion.4, f32[4,49,512]{2,1,0:T(8,128)S(1)} %get-tuple-element.75, f32[512]{0:T(512)S(1)} %get-tuple-element.71, f32[512]{0:T(512)S(1)} %get-tuple-element.70, f32[4,49]{1,0:T(4,128)S(1)} %add_rsqrt_fusion.1, f32[4,49]{1,0:T(4,128)S(1)} %broadcast_multiply_fusion.5), kind=kOutput, calls=%fused_computation.1 | convolution fusion | flops 412592128 | bytes 3307040 | tf_op jit(solution)/shard_map/wic,wif->cf/dot_general | solution.py:90
  70.0 1.3 reshape.283
  71.2 2.0 %copy.110 = bf16[4,16,49,32]{2,3,1,0:T(8,128)(2,1)S(1)} copy(bf16[4,16,49,32]{3,1,0,2:T(8,128)(2,1)} %bitcast.188) | data formatting | bytes 401408 | tf_op jit(solution)/shard_map/transpose | solution.py:81
  73.3 1.4 convolution_convert_fusion
  74.7 0.9 multiply_reduce_fusion
  75.6 1.2 fusion.18
  79.1 2.2 %multiply_reduce_fusion.2 = (bf16[512]{0:T(512)(128)(2,1)S(1)}, f32[4,49]{1,0:T(4,128)S(1)}, f32[4,49]{1,0:T(4,128)S(1)}, bf16[512]{0:T(512)(128)(2,1)S(1)}, f32[4,49,512]{2,1,0:T(8,128)S(1)}) fusion(f32[4,49,512]{2,0,1:T(4,128)S(1)} %bitcast.185, f32[4,49]{1,0:T(4,128)S(1)} %div.43, f32[4,49]{1,0:T(4,128)S(1)} %rsqrt.22, f32[512]{0:T(512)S(1)} %get-tuple-element.73, ...), kind=kOutput, calls=%fused_computation.52 | convolution fusion | flops 310989440 | bytes 2985024 | tf_op jit(solution)/shard_map/wid,cd->wic/dot_general | solution.py:90
  82.2 1.9 %fusion = bf16[512,1536]{1,0:T(8,128)(2,1)} fusion(bf16[4,49,512]{2,1,0:T(8,128)(2,1)S(1)} %copy.117, bf16[4,49,512]{2,1,0:T(8,128)(2,1)S(1)} %copy.116, bf16[4,49,512]{2,1,0:T(8,128)(2,1)S(1)} %copy.115, f32[4,49,512]{2,0,1:T(4,128)S(1)} %bitcast.187, f32[512]{0:T(512)S(1)} %get-tuple-element.72, f32[4,49]{1,0:T(4,128)S(1)} %div.43, ...), kind=kOutput, calls=%fused_computation.3 | convolution fusion | flops 311375872 | bytes 2582048 | tf_op jit(solution)/shard_map/wic,wid->cd/dot_general | solution.py:90
  84.1 2.0 %bitcast_convert_fusion = bf16[2048,512]{1,0:T(8,128)(2,1)} fusion(bf16[4,49,2048]{2,1,0:T(8,128)(2,1)S(1)} %copy-done.4, bf16[4,49,512]{2,0,1:T(4,128)(2,1)S(1)} %bitcast.221), kind=kOutput, calls=%fused_computation | convolution fusion | flops 412090368 | bytes 3100672 | tf_op jit(solution)/shard_map/wif,wic->fc/dot_general | solution.py:90
  86.3 1.4 collective-permute-start.1
  88.0 1.1 fusion.15
  90.2 66.2 %shard_map.213 = (bf16[4,2,16,2048]{3,2,1,0:T(8,128)(2,1)}, bf16[4,2,64,512]{3,2,1,0:T(8,128)(2,1)}, bf16[4,2,16,1536]{3,2,1,0:T(8,128)(2,1)}, bf16[4,2,16,512]{3,2,1,0:T(8,128)(2,1)}, bf16[4,2,16,128]{3,2,1,0:T(8,128)(2,1)}) custom-call(bf16[2,2,4,2,16,2048]{5,4,3,2,1,0:T(8,128)(2,1)} %bitcast.189, bf16[2,2,4,2,64,512]{5,4,3,2,1,0:T(8,128)(2,1)} %bitcast.190, ...), custom_call_target="tpu_custom_call" | custom-call | tf_op jit(solution)/shard_map/pallas_call | solution.py:245
  156.4 1.7 %bitcast_convert_fusion.5 = f32[128,512]{1,0:T(8,128)} fusion(bf16[4,2,16,512]{3,2,1,0:T(8,128)(2,1)} %get-tuple-element.28), kind=kLoop, calls=%fused_computation.93 | loop fusion | flops 65536 | bytes 393216 | tf_op jit(solution)/shard_map/convert_element_type | solution.py:474
  158.1 2.0 %bitcast_convert_fusion.4 = f32[128,1536]{1,0:T(8,128)} fusion(bf16[4,2,16,1536]{3,2,1,0:T(8,128)(2,1)} %get-tuple-element.27), kind=kLoop, calls=%fused_computation.67 | loop fusion | flops 196608 | bytes 1179648 | tf_op jit(solution)/shard_map/convert_element_type | solution.py:473
  160.1 1.1 bitcast_convert_fusion.3
  161.2 1.1 bitcast_convert_fusion.2
  162.3 1.3 fusion.52
  166.0 1.2 copy.126
  (139 shorter events, 20.7 us)
Async XLA Ops:
  0.6 9.4 %copy-start = (s32[56,28]{0,1:T(8,128)S(1)}, s32[56,28]{0,1:T(8,128)}, u32[]{:S(2)}) copy-start(s32[56,28]{0,1:T(8,128)} %param.15) | copy-start | bytes 18820
  0.7 49.4 %copy-start.21 = (s32[49,49]{1,0:T(8,128)S(1)}, s32[49,49]{1,0:T(8,128)}, u32[]{:S(2)}) copy-start(s32[49,49]{1,0:T(8,128)} %param.16) | copy-start | bytes 28816
  1.7 51.1 %collective-permute-start.2 = (bf16[3,28,512]{2,0,1:T(4,128)(2,1)S(1)}, bf16[3,28,512]{2,0,1:T(4,128)(2,1)S(1)}, u32[]{:S(2)}, u32[]{:S(2)}) collective-permute-start(bf16[3,28,512]{2,0,1:T(4,128)(2,1)S(1)} %bitcast.228), channel_id=1, source_target_pairs={{0,7},{1,0},{2,1},{3,2},{4,3},{5,4},{6,5},{7,6},{8,15},{9,8},{10,9... | collective-permute-start | bytes 258056 | tf_op jit(solution)/shard_map/ppermute | solution.py:339
  8.6 42.2 %slice-start.1 = ((bf16[1,7,28,512]{3,2,1,0:T(8,128)(2,1)}), bf16[1,4,28,512]{3,2,1,0:T(8,128)(2,1)S(1)}, s32[]{:S(2)}) async-start(bf16[1,7,28,512]{3,2,1,0:T(8,128)(2,1)} %param.13), calls=%async_computation.1 | async-start | bytes 262144 | tf_op jit(solution)/shard_map/slice | solution.py:340
  8.7 42.2 %slice-start = ((bf16[1,7,28,512]{3,2,1,0:T(8,128)(2,1)}), bf16[1,4,28,512]{3,2,1,0:T(8,128)(2,1)S(1)}, s32[]{:S(2)}) async-start(bf16[1,7,28,512]{3,2,1,0:T(8,128)(2,1)} %param.14), calls=%async_computation | async-start | bytes 262144 | tf_op jit(solution)/shard_map/slice | solution.py:340
  8.7 43.3 %collective-permute-start = (bf16[3,28,512]{2,0,1:T(4,128)(2,1)S(1)}, bf16[3,28,512]{2,0,1:T(4,128)(2,1)S(1)}, u32[]{:S(2)}, u32[]{:S(2)}) collective-permute-start(bf16[3,28,512]{2,0,1:T(4,128)(2,1)S(1)} %bitcast.229), channel_id=1, source_target_pairs={{0,7},{1,0},{2,1},{3,2},{4,3},{5,4},{6,5},{7,6},{8,15},{9,8},{10,9... | collective-permute-start | bytes 258056 | tf_op jit(solution)/shard_map/ppermute | solution.py:339
  52.5 1.4 copy-start.14
  52.5 1.4 copy-start.19
  53.1 11.3 %copy-start.15 = (bf16[1,4,7,7,512]{4,1,3,2,0:T(4,128)(2,1)}, bf16[1,4,7,7,512]{4,1,3,2,0:T(4,128)(2,1)S(1)}, u32[]{:S(2)}) copy-start(bf16[1,4,7,7,512]{4,1,3,2,0:T(4,128)(2,1)S(1)} %copy.105) | copy-start | bytes 602116
  53.5 5.2 %copy-start.1 = (f32[1,4,7,7,512]{4,1,3,2,0:T(4,128)}, f32[1,4,7,7,512]{4,1,3,2,0:T(4,128)S(1)}, u32[]{:S(2)}) copy-start(f32[1,4,7,7,512]{4,1,3,2,0:T(4,128)S(1)} %copy.86) | copy-start | bytes 1204228
  54.9 3.4 %copy-start.8 = (bf16[4,49,512]{1,2,0:T(8,128)(2,1)}, bf16[4,49,512]{1,2,0:T(8,128)(2,1)S(1)}, u32[]{:S(2)}) copy-start(bf16[4,49,512]{1,2,0:T(8,128)(2,1)S(1)} %copy.140) | copy-start | bytes 602116
  58.3 1.0 copy-start.5
  58.7 1.6 copy-start.7
  60.3 1.6 copy-start.6
  61.2 4.9 %copy-start.3 = (bf16[4,49,2048]{2,1,0:T(8,128)(2,1)}, bf16[4,49,2048]{2,1,0:T(8,128)(2,1)S(1)}, u32[]{:S(2)}) copy-start(bf16[4,49,2048]{2,1,0:T(8,128)(2,1)S(1)} %get-tuple-element.76) | copy-start | bytes 2408452
  75.6 1.2 copy-start.10
  76.8 1.0 copy-start.9
  76.8 1.6 copy-start.11
  77.8 1.3 copy-start.2
  82.1 2.0 %copy-start.4 = (bf16[4,49,2048]{2,1,0:T(8,128)(2,1)S(1)}, bf16[4,49,2048]{2,1,0:T(8,128)(2,1)}, u32[]{:S(2)}) copy-start(bf16[4,49,2048]{2,1,0:T(8,128)(2,1)} %copy-done.3) | copy-start | bytes 2408452
  82.2 2.0 %copy-start.16 = (bf16[1,4,7,7,512]{4,1,3,2,0:T(4,128)(2,1)S(1)}, bf16[1,4,7,7,512]{4,1,3,2,0:T(4,128)(2,1)}, u32[]{:S(2)}) copy-start(bf16[1,4,7,7,512]{4,1,3,2,0:T(4,128)(2,1)} %copy-done.15) | copy-start | bytes 602116
  84.1 2.1 %copy-start.12 = (bf16[7,25,512]{2,0,1:T(8,128)(2,1)S(1)}, bf16[7,25,512]{2,0,1:T(8,128)(2,1)}, u32[]{:S(2)}) copy-start(bf16[7,25,512]{2,0,1:T(8,128)(2,1)} %slice.155) | copy-start | bytes 537604
  84.1 3.6 %copy-start.13 = (f32[16,49,49]{1,2,0:T(8,128)S(1)}, f32[16,49,49]{1,2,0:T(8,128)}, u32[]{:S(2)}) copy-start(f32[16,49,49]{1,2,0:T(8,128)} %get-tuple-element.61) | copy-start | bytes 460996
  84.1 3.9 %copy-start.22 = (s32[49,49]{1,0:T(8,128)S(1)}, s32[49,49]{1,0:T(8,128)}, u32[]{:S(2)}) copy-start(s32[49,49]{1,0:T(8,128)} %param.16) | copy-start | bytes 28816
  86.2 3.1 %copy-start.20 = (bf16[512]{0:T(512)(128)(2,1)S(1)}, bf16[512]{0:T(512)(128)(2,1)}, u32[]{:S(2)}) copy-start(bf16[512]{0:T(512)(128)(2,1)} %get-tuple-element.53) | copy-start | bytes 3076
  86.3 78.8 %collective-permute-start.1 = (bf16[3,28,512]{2,0,1:T(4,128)(2,1)S(1)}, bf16[3,28,512]{2,0,1:T(4,128)(2,1)S(1)}, u32[]{:S(2)}, u32[]{:S(2)}) collective-permute-start(bf16[3,28,512]{2,0,1:T(4,128)(2,1)S(1)} %fusion.41), channel_id=1, source_target_pairs={{0,1},{1,2},{2,3},{3,4},{4,5},{5,6},{6,7},{7,0},{8,9},{9,10},{10,1... | collective-permute-start | bytes 258056 | tf_op jit(solution)/shard_map/ppermute | solution.py:347
  90.1 75.9 %collective-permute-start.3 = (f32[3,28,512]{2,0,1:T(4,128)S(1)}, f32[3,28,512]{2,0,1:T(4,128)S(1)}, u32[]{:S(2)}, u32[]{:S(2)}) collective-permute-start(f32[3,28,512]{2,0,1:T(4,128)S(1)} %fusion.27), channel_id=1, source_target_pairs={{0,1},{1,2},{2,3},{3,4},{4,5},{5,6},{6,7},{7,0},{8,9},{9,10},{10,1... | collective-permute-start | bytes 516104 | tf_op jit(solution)/shard_map/ppermute | solution.py:347
  156.4 3.7 %copy-start.18 = (bf16[4,2,16,2048]{3,2,1,0:T(8,128)(2,1)S(1)}, bf16[4,2,16,2048]{3,2,1,0:T(8,128)(2,1)}, u32[]{:S(2)}) copy-start(bf16[4,2,16,2048]{3,2,1,0:T(8,128)(2,1)} %get-tuple-element.29) | copy-start | bytes 1572868
  156.4 4.8 %copy-start.17 = (bf16[4,2,64,512]{3,2,1,0:T(8,128)(2,1)S(1)}, bf16[4,2,64,512]{3,2,1,0:T(8,128)(2,1)}, u32[]{:S(2)}) copy-start(bf16[4,2,64,512]{3,2,1,0:T(8,128)(2,1)} %get-tuple-element.30) | copy-start | bytes 1572868
